TPU v7x, 32 devices: a whole 2x2x4 slice. The times are simulated.
32 devices in a mesh: dp: 2 (over x), row: 4 (over z), col: 4 (over y, core).
Axes of the slice: x: 2, y: 2, z: 4, core: 2. Of those that a mesh axis runs over, the one named last changes fastest.
Arguments:
- layer_input: bfloat16 [4096, 1152], P(('dp', 'col'), 'row'), may hold values from -6 to 6
- block_ids: int32 [2, 2048], P('dp', ('row', 'col')), may hold values from 0 to 31, never falling along the last dimension, each value on 1 to 512 neighbouring positions
- positions: int32 [2, 2048], P('dp', ('row', 'col')), may hold values from 0 to 2047
- norm_attn: float32 [2, 1152], P(None, 'row'), may hold values from 0.5 to 1.5
- w_qkv: bfloat16 [2, 1152, 1920], P(None, 'row', 'col'), may hold values from -0.1875 to 0.1875
- w_out: bfloat16 [2, 1152, 1152], P(None, 'col', 'row'), may hold values from -0.75 to 0.75
- norm_ffn: float32 [2, 1152], P(None, 'row'), may hold values from 0.5 to 1.5
- w_gate_up: bfloat16 [2, 1152, 2, 3072], P(None, 'row', None, 'col'), may hold values from -0.1875 to 0.1875
- w_down: bfloat16 [2, 3072, 1152], P(None, 'col', 'row'), may hold values from -0.109375 to 0.109375
- cotangent: bfloat16 [4096, 1152], P(('dp', 'col'), 'row'), may hold values from -6 to 6
Outputs:
- activations: bfloat16 [4096, 1152], P(('dp', 'col'), 'row')
- input_grad: float32 [4096, 1152], P(('dp', 'col'), 'row')
- grad_norm_attn: float32 [2, 1152], P(None, 'row')
- grad_qkv: float32 [2, 1152, 1920], P(None, 'row', 'col')
- grad_out: float32 [2, 1152, 1152], P(None, 'col', 'row')
- grad_norm_ffn: float32 [2, 1152], P(None, 'row')
- grad_gate_up: float32 [2, 1152, 2, 3072], P(None, 'row', None, 'col')
- grad_down: float32 [2, 3072, 1152], P(None, 'col', 'row')
Inputs may be any that keep to these rules, and one draw needn't show every extreme that they name: `block_ids`: in each sequence the ids never fall, and each id covers 1 to 512 consecutive tokens.
All inputs are finite; a program needn't handle non-finite values.
Results may differ from a plain program's by a relative error of at most 0.035.
Values may be sent and summed in bfloat16 or wider, within the bound.
No kernel may reach another device: no remote copies, remote signals or barrier semaphores. Data moves between devices by JAX's collectives and lax.ppermute only.
A program may use at most 192 MiB of HBM per device.

v0:
```python
import jax
import jax.numpy as jnp
from jax import lax
from jax.sharding import PartitionSpec as P

D = 1152
HEADS = 18
KV_HEADS = 6
HEAD_DIM = 64


epsilon = 1e-05
rope_base = 10000.0


def feature_total(values):
    return lax.psum(values, "row")


def contract(left, weight, flipped):
    if flipped:
        return lax.dot_general(
            left, weight, (((1,), (1,)), ((), ())), preferred_element_type=jnp.float32
        )
    return jnp.dot(left, weight, preferred_element_type=jnp.float32)


def outer_sum(left_all, right_all):
    return lax.dot_general(
        left_all, right_all, (((0,), (0,)), ((), ())), preferred_element_type=jnp.float32
    )


def paired_einsum(form, wide, narrow):
    upper = wide.astype(jnp.bfloat16)
    lower = (wide - upper.astype(jnp.float32)).astype(jnp.bfloat16)
    return jnp.einsum(form, upper, narrow, preferred_element_type=jnp.float32) + jnp.einsum(
        form, lower, narrow, preferred_element_type=jnp.float32
    )


def gather_cols(active):
    return lax.all_gather(active, "col", axis=0, tiled=True)


def spread_cols(active, weight, flipped):
    gathered = gather_cols(active)
    share = gathered.shape[0] // lax.axis_size("row")

    def term(start, count):
        return contract(gathered, weight, flipped)

    return (
        lax.psum_scatter(
            term(jnp.int32(0), share * lax.axis_size("row")).astype(jnp.bfloat16),
            "row",
            scatter_dimension=0,
            tiled=True,
        ).astype(jnp.float32),
        gathered,
    )


def spread_rows(active, weight, flipped):
    gathered = lax.all_gather(active, "row", axis=0, tiled=True)
    share = gathered.shape[0] // lax.axis_size("col")

    def term(start, count):
        return contract(gathered, weight, flipped)

    return (
        lax.psum_scatter(
            term(jnp.int32(0), share * lax.axis_size("col")).astype(jnp.bfloat16),
            "col",
            scatter_dimension=0,
            tiled=True,
        ).astype(jnp.float32),
        gathered,
    )


def to_blocks(values):
    return lax.all_to_all(values, "col", split_axis=0, concat_axis=1, tiled=True)


def from_blocks(values):
    return lax.all_to_all(values, "col", split_axis=1, concat_axis=0, tiled=True)


def norm_scale(state):
    total = feature_total(jnp.sum(state * state, axis=1))
    return lax.rsqrt(total / D + epsilon)


def norm_backward(state, scale, gain, grad_normed, grad_state):
    inner = feature_total(jnp.sum(state * gain * grad_normed, axis=1))
    gain_grad = jnp.sum(state * scale[:, None] * grad_normed, axis=0)
    state_grad = (
        grad_state + scale[:, None] * gain * grad_normed - state * (scale**3 * inner / D)[:, None]
    )
    return (state_grad, gain_grad)


def angles(positions):
    freq_index = jnp.arange(HEAD_DIM // 2).astype(jnp.float32)
    freqs = rope_base ** (-2.0 * freq_index / HEAD_DIM)
    phase = positions.astype(jnp.float32)[:, None] * freqs[None, :]
    phase = jnp.concatenate([phase, phase], axis=-1)
    return (jnp.cos(phase)[:, None, :], jnp.sin(phase)[:, None, :])


def rotate(values, cosine, sine):
    half_dim = values.shape[-1] // 2
    turned = jnp.concatenate([-values[..., half_dim:], values[..., :half_dim]], axis=-1)
    return values * cosine + turned * sine


def key_layout(keys_all, values_all, ids_all):
    key_count = keys_all.shape[0]
    block_len = min(1024, key_count)
    blocks = key_count // block_len
    return (
        keys_all.reshape(blocks, block_len, KV_HEADS, HEAD_DIM),
        values_all.reshape(blocks, block_len, KV_HEADS, HEAD_DIM),
        ids_all.reshape(blocks, block_len),
    )


def attend_forward(queries, keys_all, values_all, ids_all, ids_own):
    query_count = queries.shape[0]
    group = HEADS // KV_HEADS
    factor = HEAD_DIM ** (-0.5)
    grouped = queries.reshape(query_count, KV_HEADS, group, HEAD_DIM)
    laid_out = key_layout(keys_all, values_all, ids_all)

    def step(carry, block_item):
        running_max, running_sum, accumulated = carry
        key_block, value_block, id_block = block_item
        scores = (
            jnp.einsum("qhgd,khd->hgqk", grouped, key_block, preferred_element_type=jnp.float32)
            * factor
        )
        allowed = id_block[None, :] <= ids_own[:, None]
        scores = jnp.where(allowed, scores, -1e30)
        new_max = jnp.maximum(running_max, jnp.max(scores, axis=-1))
        weights = jnp.where(allowed, jnp.exp(scores - new_max[..., None]), 0.0)
        shrink = jnp.exp(running_max - new_max)
        running_sum = running_sum * shrink + jnp.sum(weights, axis=-1)
        accumulated = accumulated * shrink[..., None] + paired_einsum(
            "hgqk,khd->hgqd", weights, value_block
        )
        return ((new_max, running_sum, accumulated), None)

    start_max = jnp.full((KV_HEADS, group, query_count), -1e30, jnp.float32)
    start_sum = jnp.zeros((KV_HEADS, group, query_count), jnp.float32)
    start_acc = jnp.zeros((KV_HEADS, group, query_count, HEAD_DIM), jnp.float32)
    (final_max, final_sum, accumulated), unused = lax.scan(
        step, (start_max, start_sum, start_acc), laid_out
    )
    attended = accumulated / final_sum[..., None]
    attended = jnp.transpose(attended, (2, 0, 1, 3)).reshape(query_count, HEADS * HEAD_DIM)
    return (attended, final_max + jnp.log(final_sum))


def attend_backward(
    queries, keys_all, values_all, ids_all, ids_own, attended, log_total, grad_attended
):
    query_count = queries.shape[0]
    group = HEADS // KV_HEADS
    factor = HEAD_DIM ** (-0.5)
    grouped = queries.reshape(query_count, KV_HEADS, group, HEAD_DIM)
    grad_grouped = grad_attended.reshape(query_count, KV_HEADS, group, HEAD_DIM)
    out_grouped = attended.reshape(query_count, KV_HEADS, group, HEAD_DIM)
    delta = jnp.transpose(
        jnp.sum(grad_grouped.astype(jnp.float32) * out_grouped, axis=-1), (1, 2, 0)
    )
    laid_out = key_layout(keys_all, values_all, ids_all)

    def step(accumulated, block_item):
        key_block, value_block, id_block = block_item
        scores = (
            jnp.einsum("qhgd,khd->hgqk", grouped, key_block, preferred_element_type=jnp.float32)
            * factor
        )
        allowed = id_block[None, :] <= ids_own[:, None]
        weights = jnp.where(allowed, jnp.exp(scores - log_total[..., None]), 0.0)
        dots = jnp.einsum(
            "qhgd,khd->hgqk", grad_grouped, value_block, preferred_element_type=jnp.float32
        )
        slope = weights * (dots - delta[..., None])
        accumulated = accumulated + paired_einsum("hgqk,khd->hgqd", slope, key_block) * factor
        key_term = paired_einsum("hgqk,qhgd->khd", slope, grouped) * factor
        value_term = paired_einsum("hgqk,qhgd->khd", weights, grad_grouped)
        return (accumulated, (key_term, value_term))

    start_acc = jnp.zeros((KV_HEADS, group, query_count, HEAD_DIM), jnp.float32)
    accumulated, (key_terms, value_terms) = lax.scan(step, start_acc, laid_out)
    grad_query = jnp.transpose(accumulated, (2, 0, 1, 3)).reshape(query_count, HEADS, HEAD_DIM)
    key_count = keys_all.shape[0]
    return (
        grad_query,
        key_terms.reshape(key_count, KV_HEADS * HEAD_DIM),
        value_terms.reshape(key_count, KV_HEADS * HEAD_DIM),
    )


def layer_forward(state, weights, ids_own, cosine, sine):
    gain_attn, qkv_weight, out_weight, gain_ffn, gate_up_weight, down_weight = weights
    width_q = HEADS * HEAD_DIM
    width_k = KV_HEADS * HEAD_DIM
    scale_attn = norm_scale(state)
    normed = (state * scale_attn[:, None] * gain_attn).astype(jnp.bfloat16)
    mixed_sum, normed_all = spread_cols(normed, qkv_weight, False)
    mixed = to_blocks(mixed_sum.astype(jnp.bfloat16))
    query_count = mixed.shape[0]
    queries = rotate(
        mixed[:, :width_q].astype(jnp.float32).reshape(query_count, HEADS, HEAD_DIM), cosine, sine
    )
    queries = queries.astype(jnp.bfloat16).reshape(query_count, width_q)
    keys = rotate(
        mixed[:, width_q : width_q + width_k]
        .astype(jnp.float32)
        .reshape(query_count, KV_HEADS, HEAD_DIM),
        cosine,
        sine,
    )
    keys = keys.astype(jnp.bfloat16).reshape(query_count, width_k)
    values = mixed[:, width_q + width_k :]
    keys_all, values_all, ids_all = (
        lax.all_gather(keys, ("row", "col"), axis=0, tiled=True),
        lax.all_gather(values, ("row", "col"), axis=0, tiled=True),
        lax.all_gather(ids_own, ("row", "col"), axis=0, tiled=True),
    )
    attended, log_total = attend_forward(queries, keys_all, values_all, ids_all, ids_own)
    attended_rows = from_blocks(attended.astype(jnp.bfloat16))
    branch_sum, attended_all = spread_rows(attended_rows, out_weight, False)
    hidden = state + branch_sum
    scale_ffn = norm_scale(hidden)
    normed_ffn = (hidden * scale_ffn[:, None] * gain_ffn).astype(jnp.bfloat16)
    gate_up_flat = gate_up_weight.reshape(gate_up_weight.shape[0], -1)
    gated_sum, normed_ffn_all = spread_cols(normed_ffn, gate_up_flat, False)
    gated = gated_sum.astype(jnp.bfloat16).reshape(gated_sum.shape[0], 2, -1)
    gate_part = gated[:, 0].astype(jnp.float32)
    up_part = gated[:, 1].astype(jnp.float32)
    inner = (jax.nn.silu(gate_part) * up_part).astype(jnp.bfloat16)
    down_sum, inner_all = spread_rows(inner, down_weight, False)
    record = {
        "state": state,
        "scale_attn": scale_attn,
        "normed_all": normed_all,
        "queries": queries,
        "keys": keys,
        "values": values,
        "keys_all": keys_all,
        "values_all": values_all,
        "ids_all": ids_all,
        "attended": attended,
        "log_total": log_total,
        "attended_all": attended_all,
        "hidden": hidden,
        "scale_ffn": scale_ffn,
        "normed_ffn_all": normed_ffn_all,
        "gated": gated,
        "inner_all": inner_all,
    }
    return (record, hidden + down_sum)


def layer_backward(grad_state, record, weights, ids_own, cosine, sine):
    gain_attn, qkv_weight, out_weight, gain_ffn, gate_up_weight, down_weight = weights
    grad_down_in = grad_state.astype(jnp.bfloat16)
    grad_inner, grad_down_all = spread_cols(grad_down_in, down_weight, True)
    down_grad = outer_sum(record["inner_all"], grad_down_all)
    gate_part = record["gated"][:, 0].astype(jnp.float32)
    up_part = record["gated"][:, 1].astype(jnp.float32)
    sigmoid_gate = jax.nn.sigmoid(gate_part)
    grad_gate = grad_inner * up_part * sigmoid_gate * (1.0 + gate_part * (1.0 - sigmoid_gate))
    grad_up = grad_inner * gate_part * sigmoid_gate
    grad_gated = jnp.stack([grad_gate, grad_up], axis=1).astype(jnp.bfloat16)
    grad_gated = grad_gated.reshape(grad_gated.shape[0], -1)
    gate_up_flat = gate_up_weight.reshape(gate_up_weight.shape[0], -1)
    grad_normed_ffn, grad_gated_all = spread_rows(grad_gated, gate_up_flat, True)
    gate_up_grad = outer_sum(record["normed_ffn_all"], grad_gated_all).reshape(gate_up_weight.shape)
    grad_hidden, gain_ffn_grad = norm_backward(
        record["hidden"], record["scale_ffn"], gain_ffn, grad_normed_ffn, grad_state
    )
    grad_branch = grad_hidden.astype(jnp.bfloat16)
    grad_attended_rows, grad_branch_all = spread_cols(grad_branch, out_weight, True)
    out_grad = outer_sum(record["attended_all"], grad_branch_all)
    grad_attended = to_blocks(grad_attended_rows.astype(jnp.bfloat16))
    keys_all, values_all, ids_all = (
        lax.all_gather(record["keys"], ("row", "col"), axis=0, tiled=True),
        lax.all_gather(record["values"], ("row", "col"), axis=0, tiled=True),
        lax.all_gather(ids_own, ("row", "col"), axis=0, tiled=True),
    )
    grad_query, key_terms, value_terms = attend_backward(
        record["queries"],
        keys_all,
        values_all,
        ids_all,
        ids_own,
        record["attended"],
        record["log_total"],
        grad_attended,
    )
    key_grad, value_grad = (
        lax.psum_scatter(
            key_terms.astype(jnp.bfloat16), ("row", "col"), scatter_dimension=0, tiled=True
        ).astype(jnp.float32),
        lax.psum_scatter(
            value_terms.astype(jnp.bfloat16), ("row", "col"), scatter_dimension=0, tiled=True
        ).astype(jnp.float32),
    )
    query_count = grad_query.shape[0]
    grad_query = rotate(grad_query, cosine, -sine).reshape(query_count, HEADS * HEAD_DIM)
    key_grad = rotate(key_grad.reshape(query_count, KV_HEADS, HEAD_DIM), cosine, -sine)
    key_grad = key_grad.reshape(query_count, KV_HEADS * HEAD_DIM)
    grad_mixed = jnp.concatenate([grad_query, key_grad, value_grad], axis=1).astype(jnp.bfloat16)
    grad_mixed_rows = from_blocks(grad_mixed)
    grad_normed, grad_mixed_all = spread_rows(grad_mixed_rows, qkv_weight, True)
    qkv_grad = outer_sum(record["normed_all"], grad_mixed_all)
    grad_input, gain_attn_grad = norm_backward(
        record["state"], record["scale_attn"], gain_attn, grad_normed, grad_hidden
    )
    return (
        grad_input,
        (gain_attn_grad, qkv_grad, out_grad, gain_ffn_grad, gate_up_grad, down_grad),
    )


def local(
    layer_input,
    block_ids,
    positions,
    norm_attn,
    w_qkv,
    w_out,
    norm_ffn,
    w_gate_up,
    w_down,
    cotangent,
):
    layer_count = w_qkv.shape[0]
    ids_own = block_ids[0]
    cosine, sine = angles(positions[0])
    state = layer_input.astype(jnp.float32)
    records = []
    for layer_index in range(layer_count):
        weights = (
            norm_attn[layer_index],
            w_qkv[layer_index],
            w_out[layer_index],
            norm_ffn[layer_index],
            w_gate_up[layer_index],
            w_down[layer_index],
        )
        record, state = layer_forward(state, weights, ids_own, cosine, sine)
        records.append(record)
    result = state.astype(jnp.bfloat16)
    grad_state = cotangent.astype(jnp.float32)
    collected = [None] * layer_count
    for layer_index in reversed(range(layer_count)):
        weights = (
            norm_attn[layer_index],
            w_qkv[layer_index],
            w_out[layer_index],
            norm_ffn[layer_index],
            w_gate_up[layer_index],
            w_down[layer_index],
        )
        grad_state, layer_grads = layer_backward(
            grad_state, records[layer_index], weights, ids_own, cosine, sine
        )
        collected[layer_index] = layer_grads
    stacked = [
        jnp.stack([collected[index][member] for index in range(layer_count)], axis=0)
        for member in range(6)
    ]
    gain_attn_all, qkv_all, out_all, gain_ffn_all, gate_up_all, down_all = stacked
    qkv_all, out_all, gate_up_all, down_all = (
        lax.psum(qkv_all.astype(jnp.bfloat16), "dp").astype(jnp.float32),
        lax.psum(out_all.astype(jnp.bfloat16), "dp").astype(jnp.float32),
        lax.psum(gate_up_all.astype(jnp.bfloat16), "dp").astype(jnp.float32),
        lax.psum(down_all.astype(jnp.bfloat16), "dp").astype(jnp.float32),
    )
    gain_attn_all, gain_ffn_all = lax.psum((gain_attn_all, gain_ffn_all), ("dp", "col"))
    return (
        result,
        grad_state,
        gain_attn_all,
        qkv_all,
        out_all,
        gain_ffn_all,
        gate_up_all,
        down_all,
    )


def solution(mesh):
    in_specs = (
        P(("dp", "col"), "row"),
        P("dp", ("row", "col")),
        P("dp", ("row", "col")),
        P(None, "row"),
        P(None, "row", "col"),
        P(None, "col", "row"),
        P(None, "row"),
        P(None, "row", None, "col"),
        P(None, "col", "row"),
        P(("dp", "col"), "row"),
    )
    out_specs = (
        P(("dp", "col"), "row"),
        P(("dp", "col"), "row"),
        P(None, "row"),
        P(None, "row", "col"),
        P(None, "col", "row"),
        P(None, "row"),
        P(None, "row", None, "col"),
        P(None, "col", "row"),
    )
    return jax.shard_map(local, mesh=mesh, in_specs=in_specs, out_specs=out_specs, check_vma=False)
```

profile of v0, /device:TPU:0, one launch (start us, length us, event | category | flops | bytes accessed | tf_op | source)
XLA Modules:
  0.0 2242.0 jit_solution(16402130901566368059)
XLA Ops:
  8.3 13.5 psum.98
  24.9 15.7 all-gather.22.cloned.1.call-done
  44.6 41.7 %reduce-scatter.29.cloned.1.call-done = bf16[512,480]{0,1:T(8,128)(2,1)} async-done(((bf16[2048,480]{0,1:T(8,128)(2,1)}), bf16[512,480]{0,1:T(8,128)(2,1)}) %reduce-scatter.29.cloned.1.call-update) | async-done | bytes 491536 | tf_op jit(solution)/shard_map/reduce_scatter | solution.py:54
  102.1 18.8 all-gather
  122.4 16.2 all-gather.24.cloned.1.call-done
  144.3 35.1 %all-gather.26.cloned.1.call-done = bf16[2048,384]{0,1:T(8,128)(2,1)} async-done(((bf16[128,384]{0,1:T(8,128)(2,1)}), bf16[2048,384]{0,1:T(8,128)(2,1)}) %all-gather.26.cloned.1.call-update) | async-done | bytes 1572880 | tf_op jit(solution)/shard_map/all_gather | solution.py:231
  186.3 21.2 while.60
  217.6 28.8 %all-gather.28.cloned.1.call-done = bf16[2048,288]{0,1:T(8,128)(2,1)} async-done(((bf16[512,288]{0,1:T(8,128)(2,1)}), bf16[2048,288]{0,1:T(8,128)(2,1)}) %all-gather.28.cloned.1.call-update) | async-done | bytes 1179664 | tf_op jit(solution)/shard_map/all_gather | solution.py:65
  249.6 24.9 %reduce-scatter.31.cloned.1.call-done = bf16[512,288]{0,1:T(8,128)(2,1)} async-done(((bf16[2048,288]{0,1:T(8,128)(2,1)}), bf16[512,288]{0,1:T(8,128)(2,1)}) %reduce-scatter.31.cloned.1.call-update) | async-done | bytes 294928 | tf_op jit(solution)/shard_map/reduce_scatter | solution.py:72
  291.9 12.0 all-gather.30.cloned.1.call-done
  310.6 110.9 %reduce-scatter.33.cloned.1.call-done = bf16[512,1536]{1,0:T(8,128)(2,1)} async-done(((bf16[2048,1536]{1,0:T(8,128)(2,1)}), bf16[512,1536]{1,0:T(8,128)(2,1)}) %reduce-scatter.33.cloned.1.call-update) | async-done | bytes 1572880 | tf_op jit(solution)/shard_map/reduce_scatter | solution.py:54
  430.6 64.1 %all-gather.32.cloned.1.call-done = bf16[2048,768]{1,0:T(8,128)(2,1)} async-done(((bf16[512,768]{1,0:T(8,128)(2,1)}), bf16[2048,768]{1,0:T(8,128)(2,1)}) %all-gather.32.cloned.1.call-update) | async-done | bytes 3145744 | tf_op jit(solution)/shard_map/all_gather | solution.py:65
  498.8 24.3 %reduce-scatter.35.cloned.1.call-done = bf16[512,288]{0,1:T(8,128)(2,1)} async-done(((bf16[2048,288]{0,1:T(8,128)(2,1)}), bf16[512,288]{0,1:T(8,128)(2,1)}) %reduce-scatter.35.cloned.1.call-update) | async-done | bytes 294928 | tf_op jit(solution)/shard_map/reduce_scatter | solution.py:72
  524.2 11.7 psum.100
  536.9 14.8 all-gather.34.cloned.1.call-done
  555.5 41.7 %reduce-scatter.37.cloned.1.call-done = bf16[512,480]{0,1:T(8,128)(2,1)} async-done(((bf16[2048,480]{0,1:T(8,128)(2,1)}), bf16[512,480]{0,1:T(8,128)(2,1)}) %reduce-scatter.37.cloned.1.call-update) | async-done | bytes 491536 | tf_op jit(solution)/shard_map/reduce_scatter | solution.py:54
  612.0 35.8 %all-gather.36.cloned.1.call-done = bf16[2048,384]{0,1:T(8,128)(2,1)} async-done(((bf16[128,384]{0,1:T(8,128)(2,1)}), bf16[2048,384]{0,1:T(8,128)(2,1)}) %all-gather.36.cloned.1.call-update) | async-done | bytes 1572880 | tf_op jit(solution)/shard_map/all_gather | solution.py:230
  653.5 35.1 %all-gather.38.cloned.1.call-done = bf16[2048,384]{0,1:T(8,128)(2,1)} async-done(((bf16[128,384]{0,1:T(8,128)(2,1)}), bf16[2048,384]{0,1:T(8,128)(2,1)}) %all-gather.38.cloned.1.call-update) | async-done | bytes 1572880 | tf_op jit(solution)/shard_map/all_gather | solution.py:231
  695.5 20.4 while.61
  726.5 29.0 %all-gather.40.cloned.1.call-done = bf16[2048,288]{0,1:T(8,128)(2,1)} async-done(((bf16[512,288]{0,1:T(8,128)(2,1)}), bf16[2048,288]{0,1:T(8,128)(2,1)}) %all-gather.40.cloned.1.call-update) | async-done | bytes 1179664 | tf_op jit(solution)/shard_map/all_gather | solution.py:65
  758.9 24.8 %reduce-scatter.39.cloned.1.call-done = bf16[512,288]{0,1:T(8,128)(2,1)} async-done(((bf16[2048,288]{0,1:T(8,128)(2,1)}), bf16[512,288]{0,1:T(8,128)(2,1)}) %reduce-scatter.39.cloned.1.call-update) | async-done | bytes 294928 | tf_op jit(solution)/shard_map/reduce_scatter | solution.py:72
  784.8 11.7 psum.101
  799.9 13.2 all-gather.42.cloned.1.call-done
  836.8 108.3 %reduce-scatter.41.cloned.1.call-done = bf16[512,1536]{1,0:T(8,128)(2,1)} async-done(((bf16[2048,1536]{1,0:T(8,128)(2,1)}), bf16[512,1536]{1,0:T(8,128)(2,1)}) %reduce-scatter.41.cloned.1.call-update) | async-done | bytes 1572880 | tf_op jit(solution)/shard_map/reduce_scatter | solution.py:54
  955.4 53.3 %reduce-scatter.45.cloned.1.call-done = bf16[512,768]{1,0:T(8,128)(2,1)} async-done(((bf16[2048,768]{1,0:T(8,128)(2,1)}), bf16[512,768]{1,0:T(8,128)(2,1)}) %reduce-scatter.45.cloned.1.call-update) | async-done | bytes 786448 | tf_op jit(solution)/shard_map/reduce_scatter | solution.py:54
  1016.7 115.3 %all-gather.48.cloned.1.call-done = bf16[2048,1536]{0,1:T(8,128)(2,1)} async-done(((bf16[512,1536]{0,1:T(8,128)(2,1)}), bf16[2048,1536]{0,1:T(8,128)(2,1)}) %all-gather.48.cloned.1.call-update) | async-done | bytes 6291472 | tf_op jit(solution)/shard_map/all_gather | solution.py:65
  1138.2 23.9 %reduce-scatter.47.cloned.1.call-done = bf16[512,288]{0,1:T(8,128)(2,1)} async-done(((bf16[2048,288]{0,1:T(8,128)(2,1)}), bf16[512,288]{0,1:T(8,128)(2,1)}) %reduce-scatter.47.cloned.1.call-update) | async-done | bytes 294928 | tf_op jit(solution)/shard_map/reduce_scatter | solution.py:72
  1177.8 14.5 all-gather.50.cloned.1.call-done
  1195.6 29.5 %reduce-scatter.49.cloned.1.call-done = bf16[512,288]{0,1:T(8,128)(2,1)} async-done(((bf16[2048,288]{0,1:T(8,128)(2,1)}), bf16[512,288]{0,1:T(8,128)(2,1)}) %reduce-scatter.49.cloned.1.call-update) | async-done | bytes 294928 | tf_op jit(solution)/shard_map/reduce_scatter | solution.py:54
  1239.3 33.2 %while.62 = (s32[]{:T(128)}, f32[6,3,128,64]{2,3,1,0:T(8,128)S(1)}, bf16[2,1024,6,64]{1,3,2,0:T(8,128)(2,1)}, bf16[2,1024,6,64]{1,3,2,0:T(8,128)(2,1)}, s32[2,10...) while((s32[]{:T(128)}, f32[6,3,128,64]{2,3,1,0:T(8,128)S(1)}, ...), condition=%wide.region_31.32_spmd.clone, body=%wide.region_30.31_spmd.clone.sunk | while | flops 2479161344 | bytes 121101064 | solution.py:197
  1283.6 51.4 %reduce-scatter.61.cloned.1.call-done = bf16[128,384]{1,0:T(8,128)(2,1)} async-done(((bf16[2048,384]{1,0:T(8,128)(2,1)}), bf16[128,384]{1,0:T(8,128)(2,1)}) %reduce-scatter.61.cloned.1.call-update) | async-done | bytes 98320
  1336.1 61.5 %reduce-scatter.63.cloned.1.call-done = bf16[128,384]{1,0:T(8,128)(2,1)} async-done(((bf16[2048,384]{1,0:T(8,128)(2,1)}), bf16[128,384]{1,0:T(8,128)(2,1)}) %reduce-scatter.63.cloned.1.call-update) | async-done | bytes 98320
  1411.3 41.8 %all-gather.52.cloned.1.call-done = bf16[2048,480]{0,1:T(8,128)(2,1)} async-done(((bf16[512,480]{0,1:T(8,128)(2,1)}), bf16[2048,480]{0,1:T(8,128)(2,1)}) %all-gather.52.cloned.1.call-update) | async-done | bytes 1966096 | tf_op jit(solution)/shard_map/all_gather | solution.py:65
  1456.6 60.4 %all-gather.44.cloned.1.call-done = bf16[2048,768]{1,0:T(8,128)(2,1)} async-done(((bf16[512,768]{1,0:T(8,128)(2,1)}), bf16[2048,768]{1,0:T(8,128)(2,1)}) %all-gather.44.cloned.1.call-update) | async-done | bytes 3145744 | tf_op jit(solution)/shard_map/all_gather | solution.py:65
  1521.1 23.3 %reduce-scatter.51.cloned.1.call-done = bf16[512,288]{0,1:T(8,128)(2,1)} async-done(((bf16[2048,288]{0,1:T(8,128)(2,1)}), bf16[512,288]{0,1:T(8,128)(2,1)}) %reduce-scatter.51.cloned.1.call-update) | async-done | bytes 294928 | tf_op jit(solution)/shard_map/reduce_scatter | solution.py:72
  1557.9 15.1 reduce-scatter.43.cloned.1.call-done
  1575.6 17.5 all-gather.54.cloned.1.call-done
  1598.0 60.5 %reduce-scatter.53.cloned.1.call-done = bf16[512,768]{1,0:T(8,128)(2,1)} async-done(((bf16[2048,768]{1,0:T(8,128)(2,1)}), bf16[512,768]{1,0:T(8,128)(2,1)}) %reduce-scatter.53.cloned.1.call-update) | async-done | bytes 786448 | tf_op jit(solution)/shard_map/reduce_scatter | solution.py:54
  1662.5 115.1 %all-gather.56.cloned.1.call-done = bf16[2048,1536]{0,1:T(8,128)(2,1)} async-done(((bf16[512,1536]{0,1:T(8,128)(2,1)}), bf16[2048,1536]{0,1:T(8,128)(2,1)}) %all-gather.56.cloned.1.call-update) | async-done | bytes 6291472 | tf_op jit(solution)/shard_map/all_gather | solution.py:65
  1783.5 23.9 %reduce-scatter.55.cloned.1.call-done = bf16[512,288]{0,1:T(8,128)(2,1)} async-done(((bf16[2048,288]{0,1:T(8,128)(2,1)}), bf16[512,288]{0,1:T(8,128)(2,1)}) %reduce-scatter.55.cloned.1.call-update) | async-done | bytes 294928 | tf_op jit(solution)/shard_map/reduce_scatter | solution.py:72
  1822.9 14.7 all-gather.58.cloned.1.call-done
  1840.7 29.5 %reduce-scatter.57.cloned.1.call-done = bf16[512,288]{0,1:T(8,128)(2,1)} async-done(((bf16[2048,288]{0,1:T(8,128)(2,1)}), bf16[512,288]{0,1:T(8,128)(2,1)}) %reduce-scatter.57.cloned.1.call-update) | async-done | bytes 294928 | tf_op jit(solution)/shard_map/reduce_scatter | solution.py:54
  1884.5 32.9 %while.63 = (s32[]{:T(128)}, f32[6,3,128,64]{2,3,1,0:T(8,128)S(1)}, bf16[2,1024,6,64]{1,3,2,0:T(8,128)(2,1)}, bf16[2,1024,6,64]{1,3,2,0:T(8,128)(2,1)}, s32[2,10...) while((s32[]{:T(128)}, f32[6,3,128,64]{2,3,1,0:T(8,128)S(1)}, ...), condition=%wide.region_44.45_spmd.clone, body=%wide.region_43.44_spmd.clone.sunk | while | flops 2479161344 | bytes 121101064 | solution.py:197
  1928.6 51.3 %reduce-scatter.65.cloned.1.call-done = bf16[128,384]{1,0:T(8,128)(2,1)} async-done(((bf16[2048,384]{1,0:T(8,128)(2,1)}), bf16[128,384]{1,0:T(8,128)(2,1)}) %reduce-scatter.65.cloned.1.call-update) | async-done | bytes 98320
  1981.1 61.7 %reduce-scatter.67.cloned.1.call-done = bf16[128,384]{1,0:T(8,128)(2,1)} async-done(((bf16[2048,384]{1,0:T(8,128)(2,1)}), bf16[128,384]{1,0:T(8,128)(2,1)}) %reduce-scatter.67.cloned.1.call-update) | async-done | bytes 98320
  2068.8 29.3 %all-gather.60.cloned.1.call-done = bf16[2048,480]{0,1:T(8,128)(2,1)} async-done(((bf16[512,480]{0,1:T(8,128)(2,1)}), bf16[2048,480]{0,1:T(8,128)(2,1)}) %all-gather.60.cloned.1.call-update) | async-done | bytes 1966096 | tf_op jit(solution)/shard_map/all_gather | solution.py:65
  2127.5 13.9 all-reduce
  2155.1 71.9 %all-reduce.4.cloned.1.call-done = (bf16[2,288,480]{2,1,0:T(8,128)(2,1)}, bf16[2,288,288]{2,1,0:T(8,128)(2,1)}, bf16[2,288,2,768]{3,2,1,0:T(2,128)(2,1)}, bf16[2,768,288]{1,2,0:T(8,128)(2,1)}) async-done(((bf16[2,288,480]{2,1,0:T(8,128)(2,1)}, bf16[2,288,288]{2,1,0:T(8,128)(2,1)}, bf16[2,288,2,768]{3,2,1,0:T(2,128)(2,1)}, bf16[2,768,288]{1,2,0:T(8,128)(2,1)}), (bf16[2,288,480]{2,1,0:T(8,128)(2,1)}, ...) | async-done | bytes 3538960 | tf_op jit(solution)/shard_map/psum | solution.py:381
  (573 shorter events, 512.8 us)
Async XLA Ops:
  7.2 33.5 %all-gather.22.cloned.1.call-start = ((), (), s32[]{:S(2)}) async-start(), calls=%async_computation.28 | async-start | bytes 1474560 | tf_op jit(solution)/shard_map/all_gather | solution.py:43
  22.5 513.4 %copy-start.69 = (f32[288]{0:T(512)}, f32[288]{0:T(512)S(1)}, u32[]{:S(2)}) copy-start(f32[288]{0:T(512)S(1)} %get-tuple-element.518) | copy-start | bytes 3460
  24.9 61.4 %reduce-scatter.29.cloned.1.call-start = ((), (), s32[]{:S(2)}) async-start(), calls=%async_computation.29 | async-start | bytes 2457600 | tf_op jit(solution)/shard_map/reduce_scatter | solution.py:54
  88.2 11.9 all-to-all-start
  91.7 46.9 %all-gather.24.cloned.1.call-start = ((), (), s32[]{:S(2)}) async-start(), calls=%async_computation.30 | async-start | bytes 1671168 | tf_op jit(solution)/shard_map/all_gather | solution.py:230
  92.5 519.4 %copy-start.32 = (f32[128,64]{0,1:T(8,128)}, f32[128,64]{0,1:T(8,128)S(1)}, u32[]{:S(2)}) copy-start(f32[128,64]{0,1:T(8,128)S(1)} %get-tuple-element.654) | copy-start | bytes 98308
  101.5 77.9 %all-gather.26.cloned.1.call-start = ((), (), s32[]{:S(2)}) async-start(), calls=%async_computation.31 | async-start | bytes 1671168 | tf_op jit(solution)/shard_map/all_gather | solution.py:231
  102.1 144.3 %all-gather.28.cloned.1.call-start = ((), (), s32[]{:S(2)}) async-start(), calls=%async_computation.32 | async-start | bytes 1474560 | tf_op jit(solution)/shard_map/all_gather | solution.py:65
  217.3 57.2 %reduce-scatter.31.cloned.1.call-start = ((), (), s32[]{:S(2)}) async-start(), calls=%async_computation.33 | async-start | bytes 1474560 | tf_op jit(solution)/shard_map/reduce_scatter | solution.py:72
  249.5 54.4 %all-gather.30.cloned.1.call-start = ((), (), s32[]{:S(2)}) async-start(), calls=%async_computation.34 | async-start | bytes 1474560 | tf_op jit(solution)/shard_map/all_gather | solution.py:43
  249.6 926.0 %copy-start.63 = (f32[288]{0:T(512)}, f32[288]{0:T(512)S(1)}, u32[]{:S(2)}) copy-start(f32[288]{0:T(512)S(1)} %get-tuple-element.521) | copy-start | bytes 3460
  289.1 132.4 %reduce-scatter.33.cloned.1.call-start = ((), (), s32[]{:S(2)}) async-start(), calls=%async_computation.35 | async-start | bytes 7864320 | tf_op jit(solution)/shard_map/reduce_scatter | solution.py:54
  310.6 184.1 %all-gather.32.cloned.1.call-start = ((), (), s32[]{:S(2)}) async-start(), calls=%async_computation.36 | async-start | bytes 3932160 | tf_op jit(solution)/shard_map/all_gather | solution.py:65
  430.6 92.6 %reduce-scatter.35.cloned.1.call-start = ((), (), s32[]{:S(2)}) async-start(), calls=%async_computation.37 | async-start | bytes 1474560 | tf_op jit(solution)/shard_map/reduce_scatter | solution.py:72
  498.7 52.9 %all-gather.34.cloned.1.call-start = ((), (), s32[]{:S(2)}) async-start(), calls=%async_computation.38 | async-start | bytes 1474560 | tf_op jit(solution)/shard_map/all_gather | solution.py:43
  524.2 651.4 %copy-start.4 = (f32[512,288]{0,1:T(8,128)}, f32[512,288]{0,1:T(8,128)S(1)}, u32[]{:S(2)}) copy-start(f32[512,288]{0,1:T(8,128)S(1)} %get-tuple-element.619) | copy-start | bytes 1769476
  536.8 60.4 %reduce-scatter.37.cloned.1.call-start = ((), (), s32[]{:S(2)}) async-start(), calls=%async_computation.39 | async-start | bytes 2457600 | tf_op jit(solution)/shard_map/reduce_scatter | solution.py:54
  555.4 92.4 %all-gather.36.cloned.1.call-start = ((), (), s32[]{:S(2)}) async-start(), calls=%async_computation.40 | async-start | bytes 1671168 | tf_op jit(solution)/shard_map/all_gather | solution.py:230
  610.7 77.9 %all-gather.38.cloned.1.call-start = ((), (), s32[]{:S(2)}) async-start(), calls=%async_computation.41 | async-start | bytes 1671168 | tf_op jit(solution)/shard_map/all_gather | solution.py:231
  611.3 144.3 %all-gather.40.cloned.1.call-start = ((), (), s32[]{:S(2)}) async-start(), calls=%async_computation.42 | async-start | bytes 1474560 | tf_op jit(solution)/shard_map/all_gather | solution.py:65
  726.5 57.2 %reduce-scatter.39.cloned.1.call-start = ((), (), s32[]{:S(2)}) async-start(), calls=%async_computation.43 | async-start | bytes 1474560 | tf_op jit(solution)/shard_map/reduce_scatter | solution.py:72
  758.7 54.4 %all-gather.42.cloned.1.call-start = ((), (), s32[]{:S(2)}) async-start(), calls=%async_computation.44 | async-start | bytes 1474560 | tf_op jit(solution)/shard_map/all_gather | solution.py:43
  798.3 33.7 %all-gather.46.cloned.1.call-start = ((), (), s32[]{:S(2)}) async-start(), calls=%async_computation.48 | async-start | bytes 1474560 | tf_op jit(solution)/shard_map/all_gather | solution.py:43
  798.8 146.2 %reduce-scatter.41.cloned.1.call-start = ((), (), s32[]{:S(2)}) async-start(), calls=%async_computation.45 | async-start | bytes 7864320 | tf_op jit(solution)/shard_map/reduce_scatter | solution.py:54
  820.7 188.1 %reduce-scatter.45.cloned.1.call-start = ((), (), s32[]{:S(2)}) async-start(), calls=%async_computation.49 | async-start | bytes 3932160 | tf_op jit(solution)/shard_map/reduce_scatter | solution.py:54
  836.8 295.2 %all-gather.48.cloned.1.call-start = ((), (), s32[]{:S(2)}) async-start(), calls=%async_computation.50 | async-start | bytes 7864320 | tf_op jit(solution)/shard_map/all_gather | solution.py:65
  1016.6 145.4 %reduce-scatter.47.cloned.1.call-start = ((), (), s32[]{:S(2)}) async-start(), calls=%async_computation.51 | async-start | bytes 1474560 | tf_op jit(solution)/shard_map/reduce_scatter | solution.py:72
  1138.1 54.2 %all-gather.50.cloned.1.call-start = ((), (), s32[]{:S(2)}) async-start(), calls=%async_computation.52 | async-start | bytes 1474560 | tf_op jit(solution)/shard_map/all_gather | solution.py:43
  1177.5 47.5 %reduce-scatter.49.cloned.1.call-start = ((), (), s32[]{:S(2)}) async-start(), calls=%async_computation.53 | async-start | bytes 1474560 | tf_op jit(solution)/shard_map/reduce_scatter | solution.py:54
  1226.8 9.8 all-to-all-start.4
  1230.2 104.8 %reduce-scatter.61.cloned.1.call-start = ((), (), s32[]{:S(2)}) async-start(), calls=%async_computation.64 | async-start | bytes 1671168
  1277.6 120.0 %reduce-scatter.63.cloned.1.call-start = ((), (), s32[]{:S(2)}) async-start(), calls=%async_computation.65 | async-start | bytes 1671168
  1282.8 170.4 %all-gather.52.cloned.1.call-start = ((), (), s32[]{:S(2)}) async-start(), calls=%async_computation.54 | async-start | bytes 2457600 | tf_op jit(solution)/shard_map/all_gather | solution.py:65
  1410.5 106.5 %all-gather.44.cloned.1.call-start = ((), (), s32[]{:S(2)}) async-start(), calls=%async_computation.46 | async-start | bytes 3932160 | tf_op jit(solution)/shard_map/all_gather | solution.py:65
  1411.3 133.2 %reduce-scatter.51.cloned.1.call-start = ((), (), s32[]{:S(2)}) async-start(), calls=%async_computation.55 | async-start | bytes 1474560 | tf_op jit(solution)/shard_map/reduce_scatter | solution.py:72
  1456.5 116.5 %reduce-scatter.43.cloned.1.call-start = ((), (), s32[]{:S(2)}) async-start(), calls=%async_computation.47 | async-start | bytes 1474560 | tf_op jit(solution)/shard_map/reduce_scatter | solution.py:72
  1521.1 72.0 %all-gather.54.cloned.1.call-start = ((), (), s32[]{:S(2)}) async-start(), calls=%async_computation.56 | async-start | bytes 1474560 | tf_op jit(solution)/shard_map/all_gather | solution.py:43
  1575.5 82.9 %reduce-scatter.53.cloned.1.call-start = ((), (), s32[]{:S(2)}) async-start(), calls=%async_computation.57 | async-start | bytes 3932160 | tf_op jit(solution)/shard_map/reduce_scatter | solution.py:54
  1597.9 179.7 %all-gather.56.cloned.1.call-start = ((), (), s32[]{:S(2)}) async-start(), calls=%async_computation.58 | async-start | bytes 7864320 | tf_op jit(solution)/shard_map/all_gather | solution.py:65
  1662.2 145.1 %reduce-scatter.55.cloned.1.call-start = ((), (), s32[]{:S(2)}) async-start(), calls=%async_computation.59 | async-start | bytes 1474560 | tf_op jit(solution)/shard_map/reduce_scatter | solution.py:72
  1783.4 54.2 %all-gather.58.cloned.1.call-start = ((), (), s32[]{:S(2)}) async-start(), calls=%async_computation.60 | async-start | bytes 1474560 | tf_op jit(solution)/shard_map/all_gather | solution.py:43
  1822.9 47.3 %reduce-scatter.57.cloned.1.call-start = ((), (), s32[]{:S(2)}) async-start(), calls=%async_computation.61 | async-start | bytes 1474560 | tf_op jit(solution)/shard_map/reduce_scatter | solution.py:54
  1871.9 9.8 all-to-all-start.6
  1875.4 104.5 %reduce-scatter.65.cloned.1.call-start = ((), (), s32[]{:S(2)}) async-start(), calls=%async_computation.66 | async-start | bytes 1671168
  1922.6 120.2 %reduce-scatter.67.cloned.1.call-start = ((), (), s32[]{:S(2)}) async-start(), calls=%async_computation.67 | async-start | bytes 1671168
  1927.7 170.4 %all-gather.60.cloned.1.call-start = ((), (), s32[]{:S(2)}) async-start(), calls=%async_computation.62 | async-start | bytes 2457600 | tf_op jit(solution)/shard_map/all_gather | solution.py:65
  2055.5 70.7 %reduce-scatter.59.cloned.1.call-start = ((), (), s32[]{:S(2)}) async-start(), calls=%async_computation.63 | async-start | bytes 1474560 | tf_op jit(solution)/shard_map/reduce_scatter | solution.py:72
  2101.6 125.4 %all-reduce.4.cloned.1.call-start = ((), (), s32[]{:S(2)}) async-start(), calls=%async_computation.68 | async-start | bytes 7372800 | tf_op jit(solution)/shard_map/psum | solution.py:381
  (110 other events, 3716.5 us)
Sparse Core Ops, SparseCore 0:
  25.0 15.6 all-gather.21
  44.7 41.5 reduce-scatter.28
  101.6 36.9 all-gather.23
  141.2 38.1 all-gather.25
  217.4 28.8 all-gather.27
  249.6 24.8 reduce-scatter.30
  289.2 14.6 all-gather.29
  310.7 110.7 reduce-scatter.32
  430.7 63.9 all-gather.31
  498.8 24.2 reduce-scatter.34
  536.9 14.6 all-gather.33
  555.5 41.5 reduce-scatter.36
  610.8 36.9 all-gather.35
  650.4 38.1 all-gather.37
  726.6 28.8 all-gather.39
  758.8 24.8 reduce-scatter.38
  798.4 14.6 all-gather.41
  814.5 17.4 all-gather.45
  834.3 110.7 reduce-scatter.40
  947.8 60.9 reduce-scatter.44
  1016.7 115.2 all-gather.47
  1138.2 23.7 reduce-scatter.46
  1177.7 14.6 all-gather.49
  1195.7 29.3 reduce-scatter.48
  1277.8 57.1 reduce-scatter.60
  1339.1 58.4 reduce-scatter.62
  1410.6 42.4 all-gather.51
  1454.7 62.2 all-gather.43
  1520.2 24.2 reduce-scatter.50
  1547.4 25.5 reduce-scatter.42
  1575.7 17.4 all-gather.53
  1598.0 60.3 reduce-scatter.52
  1662.3 115.2 all-gather.55
  1783.5 23.7 reduce-scatter.54
  1823.0 14.6 all-gather.57
  1840.8 29.3 reduce-scatter.56
  1922.7 57.1 reduce-scatter.64
  1984.1 58.5 reduce-scatter.66
  2055.6 42.4 all-gather.59
  2101.7 24.4 reduce-scatter.58
  2129.2 97.7 all-reduce.3
where the time goes:
time: 2250 us; the launch traced here: 2240 us
  waiting for transfers between devices  1680 us (75%)
  blocking collectives  178 us (8%)
  matrix products  177 us (8%)
  local copies, waits for them, and re-layouts  105 us (5%)
  other arithmetic  67.7 us (3%)
    all_gather x8, waiting for transfers between devices, spread_rows(): gathered = lax.all_gather(active, 'row', axis=0, tiled=True)  484 us
    reduce_scatter x8, waiting for transfers between devices, spread_cols(): lax.psum_scatter(term(jnp.int32(0), share * lax.axis_size('row')).astype(...  475 us
    unnamed x45, waiting for transfers between devices  229 us
    reduce_scatter x8, waiting for transfers between devices, spread_rows(): lax.psum_scatter(term(jnp.int32(0), share * lax.axis_size('col')).astype(...  168 us
    all_gather x8, waiting for transfers between devices, gather_cols(): return lax.all_gather(active, 'col', axis=0, tiled=True)  114 us
    psum x8, blocking collectives, feature_total(): return lax.psum(values, 'row')  95.1 us
    psum x1, waiting for transfers between devices, local(): lax.psum(qkv_all.astype(jnp.bfloat16), 'dp').astype(jnp.float32)  71.9 us
    all_gather x2, waiting for transfers between devices, layer_forward(): lax.all_gather(values, ('row', 'col'), axis=0, tiled=True)  70.2 us
  transfers between devices with their start and end apart: 44, of which 44 were waited for; matrix products, arithmetic and copies ran while one was open for 4% of the time, Pallas kernels for 0%

commit v1 on v0

v1 whole, which is shorter than its diff:
```python
import jax
import jax.numpy as jnp
from jax import lax
from jax.sharding import PartitionSpec as P

D = 1152
HEADS = 18
KV_HEADS = 6
HEAD_DIM = 64
GROUP = HEADS // KV_HEADS
WQ = HEADS * HEAD_DIM
WK = KV_HEADS * HEAD_DIM
N_ROW = 4
N_COL = 4
PAIR = 2
CORES = 2
PLANE = PAIR * N_COL

epsilon = 1e-05
rope_base = 10000.0
bf16 = jnp.bfloat16
f32 = jnp.float32


def dot(left, right, dims=((1,), (0,))):
    return lax.dot_general(left, right, (dims, ((), ())), preferred_element_type=f32)


NT = ((1,), (1,))
TN = ((0,), (0,))


def plane_swap(value, mask):
    n_dp = lax.axis_size("dp")
    pairs = []
    for d in range(n_dp):
        for c in range(N_COL):
            pairs.append((d * N_COL + c, (d ^ (mask // N_COL)) * N_COL + (c ^ (mask % N_COL))))
    return lax.ppermute(value, ("dp", "col"), pairs)


def row_shift(value, step):
    return lax.ppermute(value, "row", [(r, (r + step) % N_ROW) for r in range(N_ROW)])


CHIPS = (0, 2, 4, 6)


def plane_gather(value):
    near = [value] + [plane_swap(value, m) for m in CHIPS[1:]]
    far = [plane_swap(piece, 1) for piece in near]
    return {m: near[i] for i, m in enumerate(CHIPS)} | {m + 1: far[i] for i, m in enumerate(CHIPS)}


def plane_reduce(pieces):
    far = [plane_swap(pieces[m + 1], 1) for m in CHIPS]
    summed = [pieces[m].astype(f32) + far[i].astype(f32) for i, m in enumerate(CHIPS)]
    total = summed[0]
    for i, m in enumerate(CHIPS[1:]):
        total = total + plane_swap(summed[i + 1].astype(bf16), m).astype(f32)
    return total


def tokens_in(value, own_row):
    n = value.shape[0] // N_ROW
    parts = value.reshape(N_ROW, n, value.shape[1])
    out = jnp.zeros((N_ROW, n, value.shape[1]), value.dtype)
    out = lax.dynamic_update_index_in_dim(out, lax.dynamic_index_in_dim(parts, own_row, 0, False), own_row, 0)
    for step in range(1, N_ROW):
        sent = lax.dynamic_index_in_dim(parts, (own_row + step) % N_ROW, 0, False)
        out = lax.dynamic_update_index_in_dim(out, row_shift(sent, step), (own_row - step) % N_ROW, 0)
    return jnp.transpose(out, (1, 0, 2)).reshape(n, N_ROW * value.shape[1])


def tokens_out(value, own_row):
    n, w = value.shape[0], value.shape[1] // N_ROW
    parts = jnp.transpose(value.reshape(n, N_ROW, w), (1, 0, 2))
    out = jnp.zeros((N_ROW, n, w), value.dtype)
    out = lax.dynamic_update_index_in_dim(out, lax.dynamic_index_in_dim(parts, own_row, 0, False), own_row, 0)
    for step in range(1, N_ROW):
        sent = lax.dynamic_index_in_dim(parts, (own_row + step) % N_ROW, 0, False)
        out = lax.dynamic_update_index_in_dim(out, row_shift(sent, step), (own_row - step) % N_ROW, 0)
    return out.reshape(N_ROW * n, w)


def sequence_gather(value):
    line = [value] + [row_shift(value, step) for step in range(1, N_ROW)]
    line = jnp.stack(line, 0)
    pair = jnp.concatenate([line, plane_swap(line, 2)], 0)
    return jnp.concatenate([pair, plane_swap(pair, 1)], 0)


def sequence_reduce(terms):
    half = terms.shape[0] // 2
    pair = terms[:half].astype(f32) + plane_swap(terms[half:], 1).astype(f32)
    line = pair[: half // 2] + plane_swap(pair[half // 2 :].astype(bf16), 2).astype(f32)
    total = line[0]
    for step in range(1, N_ROW):
        total = total + row_shift(line[step].astype(bf16), N_ROW - step).astype(f32)
    return total


def sequence_order(own_row, own_col):
    rows = (own_row - jnp.arange(N_ROW)) % N_ROW
    cols = jnp.stack([own_col, own_col ^ 2, own_col ^ 1, own_col ^ 3])
    return cols[:, None] * N_ROW + rows[None, :]


def norm_scale(state):
    return lax.rsqrt(jnp.mean(state * state, axis=1, keepdims=True) + epsilon)


def norm_backward(state, scale, gain, grad_normed, grad_state):
    inner = jnp.sum(state * gain * grad_normed, axis=1, keepdims=True)
    gain_grad = jnp.sum(state * scale * grad_normed, axis=0)
    state_grad = grad_state + scale * gain * grad_normed - state * (scale**3 * inner / D)
    return (state_grad, gain_grad)


def angles(positions):
    freq_index = jnp.arange(HEAD_DIM // 2).astype(f32)
    freqs = rope_base ** (-2.0 * freq_index / HEAD_DIM)
    phase = positions.astype(f32)[:, None] * freqs[None, :]
    phase = jnp.concatenate([phase, phase], axis=-1)
    return (jnp.cos(phase)[:, None, :], jnp.sin(phase)[:, None, :])


def rotate(values, cosine, sine):
    half_dim = values.shape[-1] // 2
    turned = jnp.concatenate([-values[..., half_dim:], values[..., :half_dim]], axis=-1)
    return values * cosine + turned * sine


def attend_forward(queries, keys, values, allowed):
    factor = HEAD_DIM ** (-0.5)
    key_heads = keys.reshape(-1, KV_HEADS, HEAD_DIM)
    value_heads = values.reshape(-1, KV_HEADS, HEAD_DIM)
    scores = jnp.einsum("hqd,khd->hqk", queries, key_heads, preferred_element_type=f32) * factor
    scores = jnp.where(allowed[None], scores, -1e30)
    row_max = jnp.max(scores, axis=-1, keepdims=True)
    weights = jnp.exp(scores - row_max)
    total = jnp.sum(weights, axis=-1, keepdims=True)
    out = jnp.einsum("hqk,khd->hqd", weights.astype(bf16), value_heads, preferred_element_type=f32)
    return out / total, row_max + jnp.log(total)


def attend_backward(queries, keys, values, allowed, attended, log_total, grad_attended):
    factor = HEAD_DIM ** (-0.5)
    key_heads = keys.reshape(-1, KV_HEADS, HEAD_DIM)
    value_heads = values.reshape(-1, KV_HEADS, HEAD_DIM)
    delta = jnp.sum(grad_attended.astype(f32) * attended, axis=-1, keepdims=True)
    scores = jnp.einsum("hqd,khd->hqk", queries, key_heads, preferred_element_type=f32) * factor
    weights = jnp.where(allowed[None], jnp.exp(scores - log_total), 0.0)
    dots = jnp.einsum("hqd,khd->hqk", grad_attended, value_heads, preferred_element_type=f32)
    slope = (weights * (dots - delta)).astype(bf16)
    grad_query = jnp.einsum("hqk,khd->hqd", slope, key_heads, preferred_element_type=f32) * factor
    grad_key = jnp.einsum("hqk,hqd->khd", slope, queries, preferred_element_type=f32) * factor
    grad_value = jnp.einsum("hqk,hqd->khd", weights.astype(bf16), grad_attended, preferred_element_type=f32)
    return grad_query, grad_key.reshape(-1, WK), grad_value.reshape(-1, WK)


def to_heads(values):
    n = values.shape[0]
    grouped = values.reshape(n, KV_HEADS, GROUP, HEAD_DIM)
    return jnp.transpose(grouped, (1, 2, 0, 3)).reshape(KV_HEADS, GROUP * n, HEAD_DIM)


def from_heads(values):
    n = values.shape[1] // GROUP
    grouped = values.reshape(KV_HEADS, GROUP, n, HEAD_DIM)
    return jnp.transpose(grouped, (2, 0, 1, 3)).reshape(n, WQ)


def split_heads(values, count):
    return values.reshape(values.shape[0], count, HEAD_DIM)


def layer_forward(state, weights, allowed, cosine, sine):
    gain_attn, qkv_weight, out_weight, gain_ffn, mlp_weight = weights
    n = state.shape[0]
    ff = mlp_weight.shape[1] // 3
    scale_attn = norm_scale(state)
    normed = (state * scale_attn * gain_attn).astype(bf16)
    mixed = dot(normed, qkv_weight, NT).astype(bf16)
    keys = rotate(split_heads(mixed[:, WQ : WQ + WK].astype(f32), KV_HEADS), cosine, sine)
    keys = keys.astype(bf16).reshape(n, WK)
    keys_all = sequence_gather(keys).reshape(-1, WK)
    values_all = sequence_gather(mixed[:, WQ + WK :]).reshape(-1, WK)
    queries = rotate(split_heads(mixed[:, :WQ].astype(f32), HEADS), cosine, sine)
    queries = to_heads(queries.astype(bf16).reshape(n, WQ))
    attended, log_total = attend_forward(queries, keys_all, values_all, allowed)
    attended_b = from_heads(attended.astype(bf16))
    hidden = state + dot(attended_b, out_weight)
    scale_ffn = norm_scale(hidden)
    normed_ffn = (hidden * scale_ffn * gain_ffn).astype(bf16)
    pieces = plane_gather(normed_ffn)
    normed_all = jnp.concatenate([pieces[m] for m in range(PLANE)], 0)
    gated = dot(normed_all, mlp_weight[:, : 2 * ff]).astype(bf16)
    inner = (jax.nn.silu(gated[:, :ff].astype(f32)) * gated[:, ff:].astype(f32)).astype(bf16)
    term = dot(inner, mlp_weight[:, 2 * ff :], NT).astype(bf16)
    down = plane_reduce([term[m * n : (m + 1) * n] for m in range(PLANE)])
    record = dict(
        state=state, scale_attn=scale_attn, normed=normed, queries=queries, keys_all=keys_all,
        values_all=values_all, attended=attended, attended_b=attended_b, log_total=log_total,
        hidden=hidden, scale_ffn=scale_ffn, normed_all=normed_all, gated=gated, inner=inner,
    )
    return (record, hidden + down)


def layer_backward(grad_state, record, weights, allowed, cosine, sine, slots):
    gain_attn, qkv_weight, out_weight, gain_ffn, mlp_weight = weights
    n = grad_state.shape[0]
    ff = mlp_weight.shape[1] // 3
    pieces = plane_gather(grad_state.astype(bf16))
    grad_all = jnp.concatenate([pieces[m] for m in range(PLANE)], 0)
    grad_inner = dot(grad_all, mlp_weight[:, 2 * ff :])
    gate = record["gated"][:, :ff].astype(f32)
    up = record["gated"][:, ff:].astype(f32)
    sig = jax.nn.sigmoid(gate)
    grad_gate = grad_inner * up * sig * (1.0 + gate * (1.0 - sig))
    grad_up = grad_inner * gate * sig
    grad_gated = jnp.concatenate([grad_gate, grad_up], axis=1).astype(bf16)
    term = dot(grad_gated, mlp_weight[:, : 2 * ff], NT).astype(bf16)
    grad_normed = plane_reduce([term[m * n : (m + 1) * n] for m in range(PLANE)])
    grad_mlp = jnp.concatenate(
        [dot(record["normed_all"], grad_gated, TN), dot(grad_all, record["inner"], TN)], axis=1
    ).astype(bf16)
    grad_mlp = lax.psum_scatter(grad_mlp, "row", scatter_dimension=0, tiled=True)
    grad_hidden, gain_ffn_grad = norm_backward(
        record["hidden"], record["scale_ffn"], gain_ffn, grad_normed, grad_state
    )
    grad_branch = grad_hidden.astype(bf16)
    grad_out = dot(record["attended_b"], grad_branch, TN).astype(bf16)
    grad_attended = to_heads(dot(grad_branch, out_weight, NT).astype(bf16))
    grad_query, key_terms, value_terms = attend_backward(
        record["queries"], record["keys_all"], record["values_all"], allowed,
        record["attended"], record["log_total"], grad_attended,
    )
    blocks = N_ROW * N_COL
    key_grad = sequence_reduce(key_terms.astype(bf16).reshape(blocks, n, WK))
    value_grad = sequence_reduce(value_terms.astype(bf16).reshape(blocks, n, WK))
    grad_query = rotate(split_heads(from_heads(grad_query), HEADS), cosine, -sine).reshape(n, WQ)
    key_grad = rotate(split_heads(key_grad, KV_HEADS), cosine, -sine).reshape(n, WK)
    grad_mixed = jnp.concatenate([grad_query, key_grad, value_grad], axis=1).astype(bf16)
    grad_normed = dot(grad_mixed, qkv_weight)
    grad_qkv = dot(grad_mixed, record["normed"], TN).astype(bf16)
    grad_input, gain_attn_grad = norm_backward(
        record["state"], record["scale_attn"], gain_attn, grad_normed, grad_hidden
    )

    def scatter_attn(full):
        parts = full.reshape(PLANE, -1, D)
        mine = plane_reduce([lax.dynamic_index_in_dim(parts, slots[m], 0, False) for m in range(PLANE)])
        return lax.psum_scatter(mine.astype(bf16).T, "row", scatter_dimension=0, tiled=True)

    return (grad_input, (gain_attn_grad, gain_ffn_grad, scatter_attn(grad_qkv), scatter_attn(grad_out), grad_mlp))


def both_halves(half_grad, own_half):
    n_dp = lax.axis_size("dp")
    total = half_grad
    for step in range(1, n_dp // PAIR):
        other = lax.ppermute(half_grad, "dp", [(d, (d + PAIR * step) % n_dp) for d in range(n_dp)])
        total = (total.astype(f32) + other.astype(f32)).astype(bf16)
    other = plane_swap(total, N_COL)
    return jnp.where(own_half == 0, jnp.stack([total, other]), jnp.stack([other, total]))


def local(layer_input, block_ids, positions, norm_attn, w_qkv, w_out, norm_ffn, w_gate_up, w_down, cotangent):
    layers = w_qkv.shape[0]
    own_row = lax.axis_index("row")
    own_col = lax.axis_index("col")
    own_half = lax.axis_index("dp") % PAIR
    slot = own_col * PAIR + own_half
    slots = [(own_col ^ (m % N_COL)) * PAIR + (own_half ^ (m // N_COL)) for m in range(PLANE)]

    def take_half(value, axis):
        size = value.shape[axis] // PAIR
        return lax.dynamic_slice_in_dim(value, own_half * size, size, axis)

    attn_parts = []
    mlp_parts = []
    for i in range(layers):
        attn_part = jnp.concatenate([take_half(w_qkv[i], 1).T, take_half(w_out[i], 0)], 0)
        attn_parts.append(attn_part)
        gate_up = take_half(w_gate_up[i], 2).reshape(w_gate_up.shape[1], -1)
        mlp_parts.append(jnp.concatenate([gate_up, take_half(w_down[i], 0).T], 1))
    tokens = jnp.concatenate([block_ids, positions], 0)
    tokens_all = lax.all_gather(tokens, ("row", "col"), axis=1, tiled=True)
    state_in = tokens_in(layer_input, own_row)
    gains = lax.all_gather(jnp.concatenate([norm_attn, norm_ffn], 0), "row", axis=1, tiled=True)

    rows_qkv = w_qkv.shape[2] // PAIR
    layer_weights = []
    for i in range(layers):
        piece = lax.all_gather(attn_parts[i], "row", axis=1, tiled=True)
        mlp_weight = lax.all_gather(mlp_parts[i], "row", axis=0, tiled=True)
        pieces = plane_gather(piece)
        qkv_weight = jnp.zeros((PLANE, rows_qkv, D), bf16)
        out_weight = jnp.zeros((PLANE, piece.shape[0] - rows_qkv, D), bf16)
        for m in range(PLANE):
            qkv_weight = lax.dynamic_update_index_in_dim(qkv_weight, pieces[m][:rows_qkv], slots[m], 0)
            out_weight = lax.dynamic_update_index_in_dim(out_weight, pieces[m][rows_qkv:], slots[m], 0)
        layer_weights.append(
            (gains[i], qkv_weight.reshape(-1, D), out_weight.reshape(-1, D), gains[layers + i], mlp_weight)
        )

    n = state_in.shape[0]
    blocks = tokens_all.reshape(2, N_ROW * N_COL, n)
    own = lax.dynamic_index_in_dim(blocks, own_col * N_ROW + own_row, 1, False)
    ids_own = own[0]
    cosine, sine = angles(own[1])
    ids_all = blocks[0][sequence_order(own_row, own_col).reshape(-1)].reshape(-1)
    allowed = ids_all[None, :] <= ids_own[:, None]
    allowed = jnp.tile(allowed, (GROUP, 1))

    state = state_in.astype(f32)
    records = []
    for i in range(layers):
        record, state = layer_forward(state, layer_weights[i], allowed, cosine, sine)
        records.append(record)
    result = tokens_out(state.astype(bf16), own_row)
    grad_state = tokens_in(cotangent, own_row).astype(f32)
    collected = [None] * layers
    for i in reversed(range(layers)):
        grad_state, collected[i] = layer_backward(
            grad_state, records[i], layer_weights[i], allowed, cosine, sine, slots
        )
    input_grad = tokens_out(grad_state.astype(bf16), own_row).astype(f32)

    gain_grads = jnp.stack([collected[i][0] for i in range(layers)] + [collected[i][1] for i in range(layers)])
    gain_grads = lax.psum(gain_grads, ("dp", "row", "col"))
    gain_grads = lax.dynamic_slice_in_dim(gain_grads, own_row * (D // N_ROW), D // N_ROW, 1)

    qkv_grads, out_grads, gate_up_grads, down_grads = [], [], [], []
    width = D // N_ROW
    for i in range(layers):
        qkv = both_halves(collected[i][2], own_half)
        qkv_grads.append(jnp.transpose(qkv, (1, 0, 2)).reshape(width, -1))
        out = both_halves(collected[i][3], own_half)
        out_grads.append(jnp.transpose(out, (0, 2, 1)).reshape(-1, width))
        mlp = both_halves(collected[i][4], own_half)
        ff = mlp.shape[2] // 3
        gate_up = mlp[:, :, : 2 * ff].reshape(PAIR, width, 2, ff)
        gate_up_grads.append(jnp.transpose(gate_up, (1, 2, 0, 3)).reshape(width, 2, PAIR * ff))
        down_grads.append(jnp.transpose(mlp[:, :, 2 * ff :], (0, 2, 1)).reshape(-1, width))
    return (
        result,
        input_grad,
        gain_grads[:layers],
        jnp.stack(qkv_grads).astype(f32),
        jnp.stack(out_grads).astype(f32),
        gain_grads[layers:],
        jnp.stack(gate_up_grads).astype(f32),
        jnp.stack(down_grads).astype(f32),
    )


def solution(mesh):
    in_specs = (
        P(("dp", "col"), "row"),
        P("dp", ("row", "col")),
        P("dp", ("row", "col")),
        P(None, "row"),
        P(None, "row", "col"),
        P(None, "col", "row"),
        P(None, "row"),
        P(None, "row", None, "col"),
        P(None, "col", "row"),
        P(("dp", "col"), "row"),
    )
    out_specs = (
        P(("dp", "col"), "row"),
        P(("dp", "col"), "row"),
        P(None, "row"),
        P(None, "row", "col"),
        P(None, "col", "row"),
        P(None, "row"),
        P(None, "row", None, "col"),
        P(None, "col", "row"),
    )
    return jax.shard_map(local, mesh=mesh, in_specs=in_specs, out_specs=out_specs, check_vma=False)
```

time: 2250 us -> 1050 us (0.47)
  waiting for transfers between devices: 1680 us -> 323 us
  starting transfers between devices: 13.6 us -> 132 us
  local copies, waits for them, and re-layouts: 105 us -> 204 us
  matrix products: 177 us -> 142 us
  blocking collectives: 178 us -> 153 us
    all_gather x20 -> x2, waiting for transfers between devices: 720 us -> 0.02 us  [local(): mlp_weight = lax.all_gather(mlp_parts[i], 'row', axis=0, tiled=True)]
    reduce_scatter x16 -> x2, waiting for transfers between devices: 643 us -> 0.04 us  [layer_backward(): lax.psum_scatter(grad_mlp, 'row', scatter_dimension=0, tiled=True)]
    ppermute x0 -> x156, waiting for transfers between devices: none -> 322 us  [the longest x120 242 us: plane_swap(): return lax.ppermute(value, ('dp', 'col'), pairs)]
    unnamed x45 -> x12, waiting for transfers between devices: 229 us -> 1.44 us
    ppermute x0 -> x156, starting transfers between devices: none -> 131 us  [the longest x120 78.4 us: plane_swap(): return lax.ppermute(value, ('dp', 'col'), pairs)]
    all_gather x1 -> x4, blocking collectives: 18.8 us -> 97.9 us  [the longest x2 62.7 us: local(): piece = lax.all_gather(attn_parts[i], 'row', axis=1, tiled=True)]
    psum x1 -> x0, waiting for transfers between devices: 71.9 us -> none  [local(): lax.psum(qkv_all.astype(jnp.bfloat16), 'dp').astype(jnp.float32)]
    psum x9 -> x1, blocking collectives: 109 us -> 54.8 us  [local(): gain_grads = lax.psum(gain_grads, ('dp', 'row', 'col'))]
  transfers between devices with their start and end apart: 44 -> 164, of which waited for: 44 -> 61; matrix products, arithmetic and copies ran while one was open for 4% -> 32% of each run, Pallas kernels for 0% -> 0%
where the time goes in v1:
time: 1050 us; the launch traced here: 1040 us
  waiting for transfers between devices  323 us (31%)
  local copies, waits for them, and re-layouts  204 us (19%)
  blocking collectives  153 us (15%)
  matrix products  142 us (14%)
  starting transfers between devices  132 us (13%)
  other arithmetic  72.5 us (7%)
  between operations  17.6 us (2%)
    ppermute x120, waiting for transfers between devices, plane_swap(): return lax.ppermute(value, ('dp', 'col'), pairs)  242 us
    ppermute x36, waiting for transfers between devices, row_shift(): lax.ppermute(value, 'row', [(r, (r + step) % N_ROW) for r in range(N_ROW)])  80.1 us
    ppermute x120, starting transfers between devices, plane_swap(): return lax.ppermute(value, ('dp', 'col'), pairs)  78.4 us
    unnamed x321, local copies, waits for them, and re-layouts  65 us
    dot_general x24, matrix products, dot(): lax.dot_general(left, right, (dims, ((), ())), preferred_element_type=f32)  62.9 us
    all_gather x2, blocking collectives, local(): piece = lax.all_gather(attn_parts[i], 'row', axis=1, tiled=True)  62.7 us
    psum x1, blocking collectives, local(): gain_grads = lax.psum(gain_grads, ('dp', 'row', 'col'))  54.8 us
    ppermute x36, starting transfers between devices, row_shift(): lax.ppermute(value, 'row', [(r, (r + step) % N_ROW) for r in range(N_ROW)])  52.6 us
  transfers between devices with their start and end apart: 164, of which 61 were waited for; matrix products, arithmetic and copies ran while one was open for 32% of the time, Pallas kernels for 0%

profile of v1, /device:TPU:0, one launch (start us, length us, event | category | flops | bytes accessed | tf_op | source)
XLA Modules:
  0.0 1044.4 jit_solution(12938107704116641453)
XLA Ops:
  13.7 30.3 %all_gather.20 = bf16[384,1152]{0,1:T(8,128)(2,1)S(1)} all-gather(bf16[384,288]{0,1:T(8,128)(2,1)S(1)} %pad_maximum_fusion.16), channel_id=1, replica_groups=mesh['dp'=2,'row'=4,'col'=4] {'row'}, dimensions={1}, use_global_device_ids=true | all-gather | bytes 1105920 | tf_op jit(solution)/shard_map/all_gather | solution.py:296
  58.4 22.0 %all_gather.18 = s32[2,2048]{1,0:T(2,128)S(1)} all-gather(s32[2,128]{1,0:T(2,128)S(1)} %pad_add_fusion), channel_id=1, replica_groups=mesh['dp'=2,'row'=4,'col'=4] {'row','col'}, dimensions={1}, use_global_device_ids=true | all-gather | bytes 17408 | tf_op jit(solution)/shard_map/all_gather | solution.py:289
  81.0 13.2 %all-gather = f32[4,288,4]{1,2,0:T(4,128)S(1)} all-gather(f32[1,288,4]{1,2,0:T(4,128)S(1)} %maximum_bitcast_fusion), channel_id=1, replica_groups=mesh['dp'=2,'row'=4,'col'=4] {'row'}, dimensions={0}, use_global_device_ids=true | all-gather | bytes 23040 | tf_op jit(solution)/shard_map/all_gather | solution.py:291
  96.0 32.4 %all_gather.22 = bf16[384,1152]{0,1:T(8,128)(2,1)S(1)} all-gather(bf16[384,288]{0,1:T(8,128)(2,1)S(1)} %pad_maximum_fusion.17), channel_id=1, replica_groups=mesh['dp'=2,'row'=4,'col'=4] {'row'}, dimensions={1}, use_global_device_ids=true | all-gather | bytes 1105920 | tf_op jit(solution)/shard_map/all_gather | solution.py:296
  161.6 5.6 collective-permute-done
  167.7 4.7 collective-permute-done.1
  192.6 4.4 collective-permute-done.76
  204.2 30.5 %collective-permute-done.4 = bf16[384,1152]{1,0:T(8,128)(2,1)S(1)} collective-permute-done((bf16[384,1152]{1,0:T(8,128)(2,1)}, bf16[384,1152]{1,0:T(8,128)(2,1)S(1)}, u32[]{:S(2)}, u32[]{:S(2)}) %collective-permute-start.4) | collective-permute-done | bytes 884768 | tf_op jit(solution)/shard_map/ppermute | solution.py:39
  240.6 18.5 %collective-permute-done.35 = bf16[384,1152]{1,0:T(8,128)(2,1)} collective-permute-done((bf16[384,1152]{1,0:T(8,128)(2,1)S(1)}, bf16[384,1152]{1,0:T(8,128)(2,1)}, u32[]{:S(2)}, u32[]{:S(2)}) %collective-permute-start.35) | collective-permute-done | bytes 884768 | tf_op jit(solution)/shard_map/ppermute | solution.py:39
  315.2 5.3 collective-permute-done.13
  343.3 4.9 select_reduce_fusion.1
  348.2 5.4 fusion
  354.5 7.4 fusion.237
  372.8 5.6 collective-permute-done.25
  378.4 6.0 collective-permute-done.23
  386.7 4.6 convolution_convert_fusion.17
  403.1 10.2 collective-permute-done.29
  430.5 5.8 collective-permute-start.41
  444.9 8.5 collective-permute-done.44
  474.1 4.5 select_reduce_fusion
  478.6 5.4 fusion.2
  485.0 7.4 fusion.238
  505.0 5.0 collective-permute-done.56
  510.0 5.4 collective-permute-done.54
  521.1 4.6 convolution_convert_fusion.16
  539.4 11.4 %collective-permute-done.80 = bf16[128,1152]{1,0:T(8,128)(2,1)S(1)} collective-permute-done((bf16[128,1152]{1,0:T(8,128)(2,1)S(1)}, bf16[128,1152]{1,0:T(8,128)(2,1)S(1)}, u32[]{:S(2)}, u32[]{:S(2)}) %collective-permute-start.80) | collective-permute-done | bytes 294944 | tf_op jit(solution)/shard_map/ppermute | solution.py:39
  554.3 8.4 collective-permute-done.60
  573.9 11.8 %fusion.29 = bf16[2048,6,64]{0,2,1:T(8,128)(2,1)} fusion(f32[6,384,2048]{2,1,0:T(8,128)} %copy-done.1, f32[6,384]{1,0:T(8,128)} %log_add_fusion.1, pred[384,2048]{1,0:T(8,128)(4,1)S(1)} %bitcast.710, bf16[6,3,8,8,128]{4,3,2,1,0:T(8,128)(2,1)} %bitcast.786), kind=kOutput, calls=%fused_computation.52 | convolution fusion | flops 623640576 | bytes 21537792 | tf_op jit(solution)/shard_map/hqk,hqd->khd/dot_general | solution.py:158
  585.7 10.7 %multiply_convert_fusion.1 = bf16[6,384,2048]{2,1,0:T(8,128)(2,1)S(1)} fusion(f32[6,384,2048]{2,1,0:T(8,128)} %copy-done.1, f32[6,384]{1,0:T(8,128)S(1)} %multiply_reduce_fusion.8, f32[6,384]{1,0:T(8,128)S(1)} %copy-done.91, pred[384,2048]{1,0:T(8,128)(4,1)S(1)} %bitcast.711, bf16[2048,6,64]{0,2,1:T(8,128)(2,1)S(1)} %copy-done.43, ...), kind=kOutput, calls=%fused_computation.3 | convolution fusion | flops 632291328 | bytes 30984192 | tf_op jit(solution)/shard_map/hqd,khd->hqk/dot_general | solution.py:154
  618.8 8.1 collective-permute-done.86
  629.5 12.4 %collective-permute-done.91 = bf16[4,128,384]{1,2,0:T(8,128)(2,1)S(1)} collective-permute-done((bf16[4,128,384]{1,2,0:T(8,128)(2,1)S(1)}, bf16[4,128,384]{1,2,0:T(8,128)(2,1)S(1)}, u32[]{:S(2)}, u32[]{:S(2)}) %collective-permute-start.91) | collective-permute-done | bytes 393248 | tf_op jit(solution)/shard_map/ppermute | solution.py:39
  664.0 5.0 collective-permute-done.96
  669.1 7.1 collective-permute-done.98
  676.4 9.0 collective-permute-done.100
  707.8 9.5 collective-permute-done.104
  723.9 16.3 %collective-permute-done.132 = bf16[240,1152]{1,0:T(8,128)(2,1)S(1)} collective-permute-done((bf16[240,1152]{1,0:T(8,128)(2,1)S(1)}, bf16[240,1152]{1,0:T(8,128)(2,1)S(1)}, u32[]{:S(2)}, u32[]{:S(2)}) %collective-permute-start.132) | collective-permute-done | bytes 552992 | tf_op jit(solution)/shard_map/ppermute | solution.py:39
  756.2 9.8 collective-permute-done.140
  770.4 4.4 convolution_convert_fusion.8
  779.5 6.2 collective-permute-start.67
  786.4 9.9 collective-permute-done.65
  820.9 10.4 %fusion.26 = bf16[2048,6,64]{0,2,1:T(8,128)(2,1)} fusion(f32[6,384,2048]{2,1,0:T(8,128)} %copy-done, f32[6,384]{1,0:T(8,128)S(1)} %log_add_fusion, pred[384,2048]{1,0:T(8,128)(4,1)S(1)} %bitcast.712, bf16[6,3,8,8,128]{4,3,2,1,0:T(8,128)(2,1)S(1)} %bitcast.783), kind=kOutput, calls=%fused_computation.51 | convolution fusion | flops 623640576 | bytes 21537792 | tf_op jit(solution)/shard_map/hqk,hqd->khd/dot_general | solution.py:158
  831.4 10.7 %multiply_convert_fusion = bf16[6,384,2048]{2,1,0:T(8,128)(2,1)S(1)} fusion(f32[6,384,2048]{2,1,0:T(8,128)} %copy-done, f32[6,384]{1,0:T(8,128)S(1)} %multiply_reduce_fusion.5, f32[6,384]{1,0:T(8,128)S(1)} %log_add_fusion, pred[384,2048]{1,0:T(8,128)(4,1)S(1)} %bitcast.713, bf16[2048,6,64]{0,2,1:T(8,128)(2,1)S(1)} %copy-done.42, ...), kind=kOutput, calls=%fused_computation.1 | convolution fusion | flops 632291328 | bytes 30984192 | tf_op jit(solution)/shard_map/hqd,khd->hqk/dot_general | solution.py:154
  881.6 6.4 collective-permute-done.112
  888.1 6.1 collective-permute-done.118
  894.2 15.2 %collective-permute-done.117 = bf16[128,384]{0,1:T(8,128)(2,1)S(1)} collective-permute-done((bf16[128,384]{0,1:T(8,128)(2,1)S(1)}, bf16[128,384]{0,1:T(8,128)(2,1)S(1)}, u32[]{:S(2)}, u32[]{:S(2)}) %collective-permute-start.117) | collective-permute-done | bytes 98336 | tf_op jit(solution)/shard_map/ppermute | solution.py:43
  925.4 54.8 %psum.7 = f32[4,1152]{1,0:T(4,128)S(1)} all-reduce(f32[4,1152]{1,0:T(4,128)S(1)} %pad_maximum_fusion.23), channel_id=1, replica_groups=mesh['dp'=2,'row'=4,'col'=4] {'dp','row','col'}, use_global_device_ids=true, to_apply=%region_18.19 | all-reduce | flops 4608 | bytes 36864 | tf_op jit(solution)/shard_map/psum | solution.py:332
  995.6 12.5 %collective-permute-done.155 = bf16[288,1152]{1,0:T(8,128)(2,1)S(1)} collective-permute-done((bf16[288,1152]{1,0:T(8,128)(2,1)}, bf16[288,1152]{1,0:T(8,128)(2,1)S(1)}, u32[]{:S(2)}, u32[]{:S(2)}) %collective-permute-start.155) | collective-permute-done | bytes 663584 | tf_op jit(solution)/shard_map/ppermute | solution.py:39
  1016.7 6.6 collective-permute-done.129
  (929 shorter events, 506.8 us)
Async XLA Ops:
  7.2 379.5 %all-gather.4.cloned.1.call-start = ((), (), s32[]{:S(2)}) async-start(), calls=%async_computation.6 | async-start | bytes 3317760 | tf_op jit(solution)/shard_map/all_gather | solution.py:297
  13.1 508.0 %all-gather.6.cloned.1.call-start = ((), (), s32[]{:S(2)}) async-start(), calls=%async_computation.7 | async-start | bytes 3317760 | tf_op jit(solution)/shard_map/all_gather | solution.py:297
  45.4 219.3 %collective-permute-start.8 = (bf16[384,1152]{1,0:T(8,128)(2,1)}, bf16[384,1152]{1,0:T(8,128)(2,1)}, u32[]{:S(2)}, u32[]{:S(2)}) collective-permute-start(bf16[384,1152]{1,0:T(8,128)(2,1)} %copy.233), channel_id=1, source_target_pairs={{0,18},{1,19},{2,16},{3,17},{16,2},{17,3},{18,0},{19,1},{4,22},{5,... | collective-permute-start | bytes 2654216 | tf_op jit(solution)/shard_map/ppermute | solution.py:39
  47.7 215.1 %collective-permute-start.6 = (bf16[384,1152]{1,0:T(8,128)(2,1)}, bf16[384,1152]{1,0:T(8,128)(2,1)}, u32[]{:S(2)}, u32[]{:S(2)}) collective-permute-start(bf16[384,1152]{1,0:T(8,128)(2,1)} %copy.233), channel_id=1, source_target_pairs={{0,16},{1,17},{2,18},{3,19},{16,0},{17,1},{18,2},{19,3},{4,20},{5,... | collective-permute-start | bytes 2654216 | tf_op jit(solution)/shard_map/ppermute | solution.py:39
  48.2 153.1 %collective-permute-start.3 = (bf16[384,1152]{1,0:T(8,128)(2,1)}, bf16[384,1152]{1,0:T(8,128)(2,1)}, u32[]{:S(2)}, u32[]{:S(2)}) collective-permute-start(bf16[384,1152]{1,0:T(8,128)(2,1)} %copy.233), channel_id=1, source_target_pairs={{0,1},{1,0},{2,3},{3,2},{16,17},{17,16},{18,19},{19,18},{4,5},{5,4... | collective-permute-start | bytes 2654216 | tf_op jit(solution)/shard_map/ppermute | solution.py:39
  50.5 122.3 %collective-permute-start.2 = (bf16[128,288]{0,1:T(8,128)(2,1)S(1)}, bf16[128,288]{0,1:T(8,128)(2,1)}, u32[]{:S(2)}, u32[]{:S(2)}) collective-permute-start(bf16[128,288]{0,1:T(8,128)(2,1)S(1)} %bitcast.824), channel_id=1, source_target_pairs={{0,12},{4,0},{8,4},{12,8},{1,13},{5,1},{9,5},{13,9},{2,14},{6,2},{... | collective-permute-start | bytes 221192 | tf_op jit(solution)/shard_map/ppermute | solution.py:43
  55.5 94.7 %collective-permute-start.68 = (bf16[128,288]{0,1:T(8,128)(2,1)}, bf16[128,288]{0,1:T(8,128)(2,1)}, u32[]{:S(2)}, u32[]{:S(2)}) collective-permute-start(bf16[128,288]{0,1:T(8,128)(2,1)} %bitcast.695), channel_id=1, source_target_pairs={{0,4},{4,8},{8,12},{12,0},{1,5},{5,9},{9,13},{13,1},{2,6},{6,10},{... | collective-permute-start | bytes 221192 | tf_op jit(solution)/shard_map/ppermute | solution.py:43
  56.9 741.4 %reduce-scatter.25.cloned.1.call-start = ((), (), s32[]{:S(2)}) async-start(), calls=%async_computation.11 | async-start | bytes 737280
  191.6 43.1 %collective-permute-start.4 = (bf16[384,1152]{1,0:T(8,128)(2,1)}, bf16[384,1152]{1,0:T(8,128)(2,1)S(1)}, u32[]{:S(2)}, u32[]{:S(2)}) collective-permute-start(bf16[384,1152]{1,0:T(8,128)(2,1)} %copy.233), channel_id=1, source_target_pairs={{0,2},{1,3},{2,0},{3,1},{16,18},{17,19},{18,16},{19,17},{4,6},{5,7... | collective-permute-start | bytes 2654216 | tf_op jit(solution)/shard_map/ppermute | solution.py:39
  197.0 68.1 %collective-permute-start.39 = (bf16[384,1152]{1,0:T(8,128)(2,1)}, bf16[384,1152]{1,0:T(8,128)(2,1)}, u32[]{:S(2)}, u32[]{:S(2)}) collective-permute-start(bf16[384,1152]{1,0:T(8,128)(2,1)} %copy.250), channel_id=1, source_target_pairs={{0,18},{1,19},{2,16},{3,17},{16,2},{17,3},{18,0},{19,1},{4,22},{5,... | collective-permute-start | bytes 2654216 | tf_op jit(solution)/shard_map/ppermute | solution.py:39
  201.3 64.0 %collective-permute-start.37 = (bf16[384,1152]{1,0:T(8,128)(2,1)}, bf16[384,1152]{1,0:T(8,128)(2,1)}, u32[]{:S(2)}, u32[]{:S(2)}) collective-permute-start(bf16[384,1152]{1,0:T(8,128)(2,1)} %copy.250), channel_id=1, source_target_pairs={{0,16},{1,17},{2,18},{3,19},{16,0},{17,1},{18,2},{19,3},{4,20},{5,... | collective-permute-start | bytes 2654216 | tf_op jit(solution)/shard_map/ppermute | solution.py:39
  237.1 22.0 %collective-permute-start.35 = (bf16[384,1152]{1,0:T(8,128)(2,1)S(1)}, bf16[384,1152]{1,0:T(8,128)(2,1)}, u32[]{:S(2)}, u32[]{:S(2)}) collective-permute-start(bf16[384,1152]{1,0:T(8,128)(2,1)S(1)} %copy-done.25), channel_id=1, source_target_pairs={{0,2},{1,3},{2,0},{3,1},{16,18},{17,19},{18,16},{19,17},{4,6},{5,7... | collective-permute-start | bytes 2654216 | tf_op jit(solution)/shard_map/ppermute | solution.py:39
  262.7 239.9 %collective-permute-start.77 = (bf16[128,1152]{0,1:T(8,128)(2,1)}, bf16[128,1152]{0,1:T(8,128)(2,1)}, u32[]{:S(2)}, u32[]{:S(2)}) collective-permute-start(bf16[128,1152]{0,1:T(8,128)(2,1)} %collective-permute-done.76), channel_id=1, source_target_pairs={{0,1},{1,0},{2,3},{3,2},{16,17},{17,16},{18,19},{19,18},{4,5},{5,4... | collective-permute-start | bytes 884744 | tf_op jit(solution)/shard_map/ppermute | solution.py:39
  264.7 17.9 %collective-permute-start.36 = (bf16[384,1152]{1,0:T(8,128)(2,1)}, bf16[384,1152]{1,0:T(8,128)(2,1)}, u32[]{:S(2)}, u32[]{:S(2)}) collective-permute-start(bf16[384,1152]{1,0:T(8,128)(2,1)} %collective-permute-done.35), channel_id=1, source_target_pairs={{0,1},{1,0},{2,3},{3,2},{16,17},{17,16},{18,19},{19,18},{4,5},{5,4... | collective-permute-start | bytes 2654216 | tf_op jit(solution)/shard_map/ppermute | solution.py:39
  265.3 58.3 %collective-permute-start.40 = (bf16[384,1152]{1,0:T(8,128)(2,1)}, bf16[384,1152]{1,0:T(8,128)(2,1)}, u32[]{:S(2)}, u32[]{:S(2)}) collective-permute-start(bf16[384,1152]{1,0:T(8,128)(2,1)} %collective-permute-done.39), channel_id=1, source_target_pairs={{0,1},{1,0},{2,3},{3,2},{16,17},{17,16},{18,19},{19,18},{4,5},{5,4... | collective-permute-start | bytes 2654216 | tf_op jit(solution)/shard_map/ppermute | solution.py:39
  265.9 25.9 %collective-permute-start.38 = (bf16[384,1152]{1,0:T(8,128)(2,1)}, bf16[384,1152]{1,0:T(8,128)(2,1)}, u32[]{:S(2)}, u32[]{:S(2)}) collective-permute-start(bf16[384,1152]{1,0:T(8,128)(2,1)} %collective-permute-done.37), channel_id=1, source_target_pairs={{0,1},{1,0},{2,3},{3,2},{16,17},{17,16},{18,19},{19,18},{4,5},{5,4... | collective-permute-start | bytes 2654216 | tf_op jit(solution)/shard_map/ppermute | solution.py:39
  273.7 24.5 %collective-permute-start.16 = (bf16[128,384]{1,0:T(8,128)(2,1)}, bf16[128,384]{1,0:T(8,128)(2,1)}, u32[]{:S(2)}, u32[]{:S(2)}) collective-permute-start(bf16[128,384]{1,0:T(8,128)(2,1)} %get-tuple-element.136), channel_id=1, source_target_pairs={{0,8},{4,12},{8,0},{12,4},{1,9},{5,13},{9,1},{13,5},{2,10},{6,14},... | collective-permute-start | bytes 294920 | tf_op jit(solution)/shard_map/ppermute | solution.py:43
  303.3 18.1 %collective-permute-start.18 = (bf16[4,128,384]{2,1,0:T(8,128)(2,1)S(1)}, bf16[4,128,384]{2,1,0:T(8,128)(2,1)S(1)}, u32[]{:S(2)}, u32[]{:S(2)}) collective-permute-start(bf16[4,128,384]{2,1,0:T(8,128)(2,1)S(1)} %pad_maximum_fusion.13), channel_id=1, source_target_pairs={{0,2},{1,3},{2,0},{3,1},{16,18},{17,19},{18,16},{19,17},{4,6},{5,7... | collective-permute-start | bytes 1179656 | tf_op jit(solution)/shard_map/ppermute | solution.py:39
  436.4 18.0 %collective-permute-start.49 = (bf16[4,128,384]{2,1,0:T(8,128)(2,1)S(1)}, bf16[4,128,384]{2,1,0:T(8,128)(2,1)S(1)}, u32[]{:S(2)}, u32[]{:S(2)}) collective-permute-start(bf16[4,128,384]{2,1,0:T(8,128)(2,1)S(1)} %pad_maximum_fusion.15), channel_id=1, source_target_pairs={{0,2},{1,3},{2,0},{3,1},{16,18},{17,19},{18,16},{19,17},{4,6},{5,7... | collective-permute-start | bytes 1179656 | tf_op jit(solution)/shard_map/ppermute | solution.py:39
  532.5 21.7 %collective-permute-start.58 = (bf16[128,1152]{1,0:T(8,128)(2,1)S(1)}, bf16[128,1152]{1,0:T(8,128)(2,1)S(1)}, u32[]{:S(2)}, u32[]{:S(2)}) collective-permute-start(bf16[128,1152]{1,0:T(8,128)(2,1)S(1)} %get-tuple-element.89), channel_id=1, source_target_pairs={{0,1},{1,0},{2,3},{3,2},{16,17},{17,16},{18,19},{19,18},{4,5},{5,4... | collective-permute-start | bytes 884744 | tf_op jit(solution)/shard_map/ppermute | solution.py:39
  538.4 24.3 %collective-permute-start.60 = (bf16[128,1152]{1,0:T(8,128)(2,1)S(1)}, bf16[128,1152]{1,0:T(8,128)(2,1)S(1)}, u32[]{:S(2)}, u32[]{:S(2)}) collective-permute-start(bf16[128,1152]{1,0:T(8,128)(2,1)S(1)} %get-tuple-element.93), channel_id=1, source_target_pairs={{0,2},{1,3},{2,0},{3,1},{16,18},{17,19},{18,16},{19,17},{4,6},{5,7... | collective-permute-start | bytes 884744 | tf_op jit(solution)/shard_map/ppermute | solution.py:39
  614.4 80.0 %collective-permute-start.146 = (bf16[144,1152]{1,0:T(8,128)(2,1)S(1)}, bf16[144,1152]{1,0:T(8,128)(2,1)S(1)}, u32[]{:S(2)}, u32[]{:S(2)}) collective-permute-start(bf16[144,1152]{1,0:T(8,128)(2,1)S(1)} %get-tuple-element.68), channel_id=1, source_target_pairs={{0,1},{1,0},{2,3},{3,2},{16,17},{17,16},{18,19},{19,18},{4,5},{5,4... | collective-permute-start | bytes 995336 | tf_op jit(solution)/shard_map/ppermute | solution.py:39
  616.2 78.5 %collective-permute-start.148 = (bf16[144,1152]{1,0:T(8,128)(2,1)S(1)}, bf16[144,1152]{1,0:T(8,128)(2,1)S(1)}, u32[]{:S(2)}, u32[]{:S(2)}) collective-permute-start(bf16[144,1152]{1,0:T(8,128)(2,1)S(1)} %get-tuple-element.72), channel_id=1, source_target_pairs={{0,2},{1,3},{2,0},{3,1},{16,18},{17,19},{18,16},{19,17},{4,6},{5,7... | collective-permute-start | bytes 995336 | tf_op jit(solution)/shard_map/ppermute | solution.py:39
  617.7 24.2 %collective-permute-start.91 = (bf16[4,128,384]{1,2,0:T(8,128)(2,1)S(1)}, bf16[4,128,384]{1,2,0:T(8,128)(2,1)S(1)}, u32[]{:S(2)}, u32[]{:S(2)}) collective-permute-start(bf16[4,128,384]{1,2,0:T(8,128)(2,1)S(1)} %slice.1010), channel_id=1, source_target_pairs={{0,2},{1,3},{2,0},{3,1},{16,18},{17,19},{18,16},{19,17},{4,6},{5,7... | collective-permute-start | bytes 1179656 | tf_op jit(solution)/shard_map/ppermute | solution.py:39
  627.1 19.7 %collective-permute-start.89 = (bf16[128,384]{0,1:T(8,128)(2,1)S(1)}, bf16[128,384]{0,1:T(8,128)(2,1)S(1)}, u32[]{:S(2)}, u32[]{:S(2)}) collective-permute-start(bf16[128,384]{0,1:T(8,128)(2,1)S(1)} %get-tuple-element.146), channel_id=1, source_target_pairs={{0,4},{4,8},{8,12},{12,0},{1,5},{5,9},{9,13},{13,1},{2,6},{6,10},{... | collective-permute-start | bytes 294920 | tf_op jit(solution)/shard_map/ppermute | solution.py:43
  650.9 44.0 %collective-permute-start.152 = (bf16[144,1152]{1,0:T(8,128)(2,1)S(1)}, bf16[144,1152]{1,0:T(8,128)(2,1)S(1)}, u32[]{:S(2)}, u32[]{:S(2)}) collective-permute-start(bf16[144,1152]{1,0:T(8,128)(2,1)S(1)} %get-tuple-element.73), channel_id=1, source_target_pairs={{0,18},{1,19},{2,16},{3,17},{16,2},{17,3},{18,0},{19,1},{4,22},{5,... | collective-permute-start | bytes 995336 | tf_op jit(solution)/shard_map/ppermute | solution.py:39
  697.8 157.1 %reduce-scatter.21.cloned.1.call-start = ((), (), s32[]{:S(2)}) async-start(), calls=%async_computation.9 | async-start | bytes 737280
  698.7 24.8 %collective-permute-start.130 = (bf16[240,1152]{1,0:T(8,128)(2,1)}, bf16[240,1152]{1,0:T(8,128)(2,1)S(1)}, u32[]{:S(2)}, u32[]{:S(2)}) collective-permute-start(bf16[240,1152]{1,0:T(8,128)(2,1)} %get-tuple-element.50), channel_id=1, source_target_pairs={{0,1},{1,0},{2,3},{3,2},{16,17},{17,16},{18,19},{19,18},{4,5},{5,4... | collective-permute-start | bytes 1658888 | tf_op jit(solution)/shard_map/ppermute | solution.py:39
  702.2 17.7 %collective-permute-start.108 = (bf16[128,1152]{1,0:T(8,128)(2,1)S(1)}, bf16[128,1152]{1,0:T(8,128)(2,1)S(1)}, u32[]{:S(2)}, u32[]{:S(2)}) collective-permute-start(bf16[128,1152]{1,0:T(8,128)(2,1)S(1)} %get-tuple-element.80), channel_id=1, source_target_pairs={{0,18},{1,19},{2,16},{3,17},{16,2},{17,3},{18,0},{19,1},{4,22},{5,... | collective-permute-start | bytes 884744 | tf_op jit(solution)/shard_map/ppermute | solution.py:39
  706.7 33.6 %collective-permute-start.132 = (bf16[240,1152]{1,0:T(8,128)(2,1)S(1)}, bf16[240,1152]{1,0:T(8,128)(2,1)S(1)}, u32[]{:S(2)}, u32[]{:S(2)}) collective-permute-start(bf16[240,1152]{1,0:T(8,128)(2,1)S(1)} %get-tuple-element.54), channel_id=1, source_target_pairs={{0,2},{1,3},{2,0},{3,1},{16,18},{17,19},{18,16},{19,17},{4,6},{5,7... | collective-permute-start | bytes 1658888 | tf_op jit(solution)/shard_map/ppermute | solution.py:39
  717.3 22.9 %collective-permute-start.136 = (bf16[240,1152]{1,0:T(8,128)(2,1)S(1)}, bf16[240,1152]{1,0:T(8,128)(2,1)S(1)}, u32[]{:S(2)}, u32[]{:S(2)}) collective-permute-start(bf16[240,1152]{1,0:T(8,128)(2,1)S(1)} %get-tuple-element.55), channel_id=1, source_target_pairs={{0,18},{1,19},{2,16},{3,17},{16,2},{17,3},{18,0},{19,1},{4,22},{5,... | collective-permute-start | bytes 1658888 | tf_op jit(solution)/shard_map/ppermute | solution.py:39
  719.9 22.9 %collective-permute-start.134 = (bf16[240,1152]{1,0:T(8,128)(2,1)S(1)}, bf16[240,1152]{1,0:T(8,128)(2,1)S(1)}, u32[]{:S(2)}, u32[]{:S(2)}) collective-permute-start(bf16[240,1152]{1,0:T(8,128)(2,1)S(1)} %get-tuple-element.56), channel_id=1, source_target_pairs={{0,16},{1,17},{2,18},{3,19},{16,0},{17,1},{18,2},{19,3},{4,20},{5,... | collective-permute-start | bytes 1658888 | tf_op jit(solution)/shard_map/ppermute | solution.py:39
  723.4 23.9 %collective-permute-start.143 = (bf16[144,1152]{1,0:T(8,128)(2,1)}, bf16[144,1152]{1,0:T(8,128)(2,1)}, u32[]{:S(2)}, u32[]{:S(2)}) collective-permute-start(bf16[144,1152]{1,0:T(8,128)(2,1)} %get-tuple-element.62), channel_id=1, source_target_pairs={{0,1},{1,0},{2,3},{3,2},{16,17},{17,16},{18,19},{19,18},{4,5},{5,4... | collective-permute-start | bytes 995336 | tf_op jit(solution)/shard_map/ppermute | solution.py:39
  723.4 23.9 %collective-permute-start.141 = (bf16[144,1152]{1,0:T(8,128)(2,1)}, bf16[144,1152]{1,0:T(8,128)(2,1)}, u32[]{:S(2)}, u32[]{:S(2)}) collective-permute-start(bf16[144,1152]{1,0:T(8,128)(2,1)} %get-tuple-element.63), channel_id=1, source_target_pairs={{0,1},{1,0},{2,3},{3,2},{16,17},{17,16},{18,19},{19,18},{4,5},{5,4... | collective-permute-start | bytes 995336 | tf_op jit(solution)/shard_map/ppermute | solution.py:39
  747.1 233.7 %reduce-scatter.23.cloned.1.call-start = ((), (), s32[]{:S(2)}) async-start(), calls=%async_computation.10 | async-start | bytes 737280
  770.3 219.7 %reduce-scatter.29.cloned.1.call-start = ((), (), s32[]{:S(2)}) async-start(), calls=%async_computation.13 | async-start | bytes 3317760 | tf_op jit(solution)/shard_map/reduce_scatter | solution.py:228
  778.3 215.6 %reduce-scatter.27.cloned.1.call-start = ((), (), s32[]{:S(2)}) async-start(), calls=%async_computation.12 | async-start | bytes 3317760 | tf_op jit(solution)/shard_map/reduce_scatter | solution.py:228
  779.5 18.6 %collective-permute-start.67 = (bf16[128,288]{0,1:T(8,128)(2,1)S(1)}, bf16[128,288]{0,1:T(8,128)(2,1)S(1)}, u32[]{:S(2)}, u32[]{:S(2)}) collective-permute-start(bf16[128,288]{0,1:T(8,128)(2,1)S(1)} %get-tuple-element.166), channel_id=1, source_target_pairs={{0,12},{4,0},{8,4},{12,8},{1,13},{5,1},{9,5},{13,9},{2,14},{6,2},{... | collective-permute-start | bytes 221192 | tf_op jit(solution)/shard_map/ppermute | solution.py:43
  814.1 195.6 %reduce-scatter.19.cloned.1.call-start = ((), (), s32[]{:S(2)}) async-start(), calls=%async_computation.8 | async-start | bytes 737280
  874.9 19.3 %collective-permute-start.118 = (bf16[128,384]{0,1:T(8,128)(2,1)S(1)}, bf16[128,384]{0,1:T(8,128)(2,1)S(1)}, u32[]{:S(2)}, u32[]{:S(2)}) collective-permute-start(bf16[128,384]{0,1:T(8,128)(2,1)S(1)} %get-tuple-element.143), channel_id=1, source_target_pairs={{0,4},{4,8},{8,12},{12,0},{1,5},{5,9},{9,13},{13,1},{2,6},{6,10},{... | collective-permute-start | bytes 294920 | tf_op jit(solution)/shard_map/ppermute | solution.py:43
  879.7 29.7 %collective-permute-start.117 = (bf16[128,384]{0,1:T(8,128)(2,1)S(1)}, bf16[128,384]{0,1:T(8,128)(2,1)S(1)}, u32[]{:S(2)}, u32[]{:S(2)}) collective-permute-start(bf16[128,384]{0,1:T(8,128)(2,1)S(1)} %get-tuple-element.144), channel_id=1, source_target_pairs={{0,8},{4,12},{8,0},{12,4},{1,9},{5,13},{9,1},{13,5},{2,10},{6,14},... | collective-permute-start | bytes 294920 | tf_op jit(solution)/shard_map/ppermute | solution.py:43
  914.4 67.5 %collective-permute-start.122 = (bf16[240,1152]{1,0:T(8,128)(2,1)}, bf16[240,1152]{1,0:T(8,128)(2,1)S(1)}, u32[]{:S(2)}, u32[]{:S(2)}) collective-permute-start(bf16[240,1152]{1,0:T(8,128)(2,1)} %get-tuple-element.43), channel_id=1, source_target_pairs={{0,1},{1,0},{2,3},{3,2},{16,17},{17,16},{18,19},{19,18},{4,5},{5,4... | collective-permute-start | bytes 1658888 | tf_op jit(solution)/shard_map/ppermute | solution.py:39
  919.0 63.1 %collective-permute-start.124 = (bf16[240,1152]{1,0:T(8,128)(2,1)}, bf16[240,1152]{1,0:T(8,128)(2,1)S(1)}, u32[]{:S(2)}, u32[]{:S(2)}) collective-permute-start(bf16[240,1152]{1,0:T(8,128)(2,1)} %get-tuple-element.47), channel_id=1, source_target_pairs={{0,2},{1,3},{2,0},{3,1},{16,18},{17,19},{18,16},{19,17},{4,6},{5,7... | collective-permute-start | bytes 1658888 | tf_op jit(solution)/shard_map/ppermute | solution.py:39
  920.0 64.2 %collective-permute-start.128 = (bf16[240,1152]{1,0:T(8,128)(2,1)}, bf16[240,1152]{1,0:T(8,128)(2,1)S(1)}, u32[]{:S(2)}, u32[]{:S(2)}) collective-permute-start(bf16[240,1152]{1,0:T(8,128)(2,1)} %get-tuple-element.48), channel_id=1, source_target_pairs={{0,18},{1,19},{2,16},{3,17},{16,2},{17,3},{18,0},{19,1},{4,22},{5,... | collective-permute-start | bytes 1658888 | tf_op jit(solution)/shard_map/ppermute | solution.py:39
  922.1 64.4 %collective-permute-start.126 = (bf16[240,1152]{1,0:T(8,128)(2,1)S(1)}, bf16[240,1152]{1,0:T(8,128)(2,1)S(1)}, u32[]{:S(2)}, u32[]{:S(2)}) collective-permute-start(bf16[240,1152]{1,0:T(8,128)(2,1)S(1)} %get-tuple-element.49), channel_id=1, source_target_pairs={{0,16},{1,17},{2,18},{3,19},{16,0},{17,1},{18,2},{19,3},{4,20},{5,... | collective-permute-start | bytes 1658888 | tf_op jit(solution)/shard_map/ppermute | solution.py:39
  923.2 68.7 %collective-permute-start.121 = (bf16[128,288]{0,1:T(8,128)(2,1)}, bf16[128,288]{0,1:T(8,128)(2,1)S(1)}, u32[]{:S(2)}, u32[]{:S(2)}) collective-permute-start(bf16[128,288]{0,1:T(8,128)(2,1)} %get-tuple-element.159), channel_id=1, source_target_pairs={{0,12},{4,0},{8,4},{12,8},{1,13},{5,1},{9,5},{13,9},{2,14},{6,2},{... | collective-permute-start | bytes 221192 | tf_op jit(solution)/shard_map/ppermute | solution.py:43
  990.0 18.1 %collective-permute-start.155 = (bf16[288,1152]{1,0:T(8,128)(2,1)}, bf16[288,1152]{1,0:T(8,128)(2,1)S(1)}, u32[]{:S(2)}, u32[]{:S(2)}) collective-permute-start(bf16[288,1152]{1,0:T(8,128)(2,1)} %reduce-scatter.29.cloned.1.call-done), channel_id=1, source_target_pairs={{0,16},{1,17},{2,18},{3,19},{16,0},{17,1},{18,2},{19,3},{4,20},{5,... | collective-permute-start | bytes 1990664 | tf_op jit(solution)/shard_map/ppermute | solution.py:39
  993.9 32.4 %collective-permute-start.154 = (bf16[288,1152]{1,0:T(8,128)(2,1)}, bf16[288,1152]{1,0:T(8,128)(2,1)}, u32[]{:S(2)}, u32[]{:S(2)}) collective-permute-start(bf16[288,1152]{1,0:T(8,128)(2,1)} %reduce-scatter.27.cloned.1.call-done), channel_id=1, source_target_pairs={{0,16},{1,17},{2,18},{3,19},{16,0},{17,1},{18,2},{19,3},{4,20},{5,... | collective-permute-start | bytes 1990664 | tf_op jit(solution)/shard_map/ppermute | solution.py:39
  (242 other events, 2700.7 us)
Sparse Core Ops, SparseCore 0:
  13.2 67.7 all-gather.3
  82.5 70.5 all-gather.5
  697.9 26.0 reduce-scatter.24
  747.3 25.9 reduce-scatter.20
  775.4 24.2 reduce-scatter.22
  802.4 51.8 reduce-scatter.28
  856.6 64.8 reduce-scatter.26
  989.2 20.5 reduce-scatter.18
